TPU v7x, 512 devices: a whole 4x8x8 slice. The times are simulated.
512 devices in a mesh: wide: 64 (over y_lo, x, z), narrow: 8 (over y_hi, core).
Axes of the slice: x: 4, y: 8 (y_hi: 4, y_lo: 2; y = y_hi * 2 + y_lo), z: 8, core: 2. Of those that a mesh axis runs over, the one named last changes fastest.
Arguments:
- alignment_rows: bfloat16 [128, 512, 256], P('wide', 'narrow'), may hold values from -6 to 6
- pair_output_gradient: bfloat16 [512, 512, 128], P('wide', 'narrow'), may hold values from -6 to 6
- layer_norm_gain: float32 [256], replicated, may hold values from 0.5 to 1.5
- layer_norm_bias: float32 [256], replicated, may hold values from -3 to 3
- projection_weight: bfloat16 [2, 256, 32], replicated, may hold values from -0.375 to 0.375
- projection_bias: float32 [2, 32], replicated, may hold values from -3 to 3
- output_weight: bfloat16 [1024, 128], replicated, may hold values from -0.1875 to 0.1875
Outputs:
- alignment_gradient: bfloat16 [128, 512, 256], P('wide', 'narrow')
- projection_gradient: float32 [2, 256, 32], replicated
- projection_bias_gradient: float32 [2, 32], replicated
- output_weight_gradient: float32 [1024, 128], replicated
- layer_norm_gradient: float32 [2, 256], replicated
All inputs are finite; a program needn't handle non-finite values.
Results may differ from a plain program's by a relative error of at most 0.012.
Values may be sent and summed in bfloat16 or wider, within the bound.
A program may use at most 64 MiB of HBM per device.

v0:
```python
import jax
import jax.numpy as jnp
from jax import lax
from jax.sharding import PartitionSpec as P

FACTOR_CHANNELS = 32
PAIR_WIDTH = 128
OUTER = 1024


def in_order(pieces, dim):
    pieces = jnp.moveaxis(pieces, 0, dim)
    lengths = pieces.shape
    return pieces.reshape(*lengths[:dim], lengths[dim] * lengths[dim + 1], *lengths[dim + 2 :])


def copy_for_each(array, axis):
    copies = jnp.broadcast_to(array, (lax.axis_size(axis), *array.shape))
    return lax.all_to_all(copies, axis, split_axis=0, concat_axis=0, tiled=True)


def gather_directly(array, axis, dim):
    return in_order(copy_for_each(array, axis), dim)


def in_blocks(array, dim, length):
    lengths = array.shape
    pieces = array.reshape(*lengths[:dim], length, lengths[dim] // length, *lengths[dim + 1 :])
    return jnp.moveaxis(pieces, dim, 0)


def sum_at_owner(array, axis, dim):
    pieces = in_blocks(array, dim, lax.axis_size(axis))
    arrived = lax.all_to_all(pieces, axis, split_axis=0, concat_axis=0, tiled=True)
    return arrived.sum(axis=0)


def summed_on_arrival(array, axis, dim):
    pieces = in_blocks(array, dim, lax.axis_size(axis))
    arrived = lax.all_to_all(pieces, axis, split_axis=0, concat_axis=0, tiled=True)
    return arrived.astype(jnp.float32).sum(axis=0)


def shards(
    alignment_rows,
    pair_output_gradient,
    layer_norm_gain,
    layer_norm_bias,
    projection_weight,
    projection_bias,
    output_weight,
):
    sequence_deviation = alignment_rows.shape[0]
    column_residue = alignment_rows.shape[1]
    row_res = pair_output_gradient.shape[0]
    total_seq = sequence_deviation * lax.axis_size("wide")
    value_rows = alignment_rows.astype(jnp.float32)
    centre = value_rows - jnp.mean(value_rows, axis=-1, keepdims=True)
    inverse_deviation = lax.rsqrt(jnp.mean(centre * centre, axis=-1, keepdims=True) + 1e-05)
    normalized_rows = centre * inverse_deviation
    scaled_product = (normalized_rows * layer_norm_gain + layer_norm_bias).astype(jnp.bfloat16)
    factors = jnp.einsum(
        "src,kch->kshr", scaled_product, projection_weight, preferred_element_type=jnp.float32
    )
    factors = (factors + projection_bias[:, None, :, None]).astype(jnp.bfloat16)
    row_factor = factors[0]
    col_factor = factors[1]
    row_local = gather_directly(row_factor, "narrow", 2)
    row_regrouped = lax.all_to_all(row_local, "wide", split_axis=2, concat_axis=0, tiled=True)
    col_whole = gather_directly(col_factor, "wide", 0)
    block_rows = row_res // 4
    weight_acc = jnp.zeros((OUTER, PAIR_WIDTH), jnp.float32)
    row_parts = []
    upstream_blocks = []
    for block_index in range(4):
        row_slice = row_regrouped[:, :, block_index * block_rows : (block_index + 1) * block_rows]
        grad_block = pair_output_gradient[
            block_index * block_rows : (block_index + 1) * block_rows
        ].reshape(block_rows * column_residue, PAIR_WIDTH)
        outer_prod = jnp.einsum(
            "spi,sqj->ijpq", row_slice, col_whole, preferred_element_type=jnp.float32
        )
        outer_b = (
            (outer_prod / total_seq)
            .astype(jnp.bfloat16)
            .reshape(block_rows * column_residue, OUTER)
        )
        weight_acc = weight_acc + jnp.einsum(
            "nk,ne->ke", outer_b, grad_block, preferred_element_type=jnp.float32
        )
        upstream = jnp.einsum(
            "ne,ke->nk", grad_block, output_weight, preferred_element_type=jnp.float32
        )
        upstream = upstream.astype(jnp.bfloat16).reshape(
            block_rows, column_residue, FACTOR_CHANNELS, FACTOR_CHANNELS
        )
        row_part = jnp.einsum(
            "ijpq,sqj->spi", upstream, col_whole, preferred_element_type=jnp.float32
        )
        row_parts.append(row_part / total_seq)
        upstream_blocks.append(upstream)
    row_partial = jnp.concatenate(row_parts, axis=2)
    upstream_all = jnp.concatenate(upstream_blocks, axis=0)
    col_grad = sum_at_owner(
        jnp.einsum("ijpq,spi->sqj", upstream_all, row_regrouped, preferred_element_type=jnp.float32)
        / total_seq,
        "wide",
        0,
    )
    moved_rows = lax.all_to_all(
        row_partial.astype(jnp.bfloat16), "wide", split_axis=0, concat_axis=2, tiled=True
    ).astype(row_partial.dtype)
    row_grad = summed_on_arrival(moved_rows.astype(jnp.bfloat16), "narrow", 2)
    factor_grad = jnp.stack([row_grad, col_grad])
    factor_grad_b = factor_grad.astype(jnp.bfloat16)
    scaled_product_gradient = jnp.einsum(
        "kshr,kch->src", factor_grad_b, projection_weight, preferred_element_type=jnp.float32
    )
    proj_local = jnp.einsum(
        "src,kshr->kch", scaled_product, factor_grad_b, preferred_element_type=jnp.float32
    )
    bias_local = jnp.sum(factor_grad, axis=(1, 3))
    norm_local = jnp.stack(
        [
            jnp.sum(scaled_product_gradient * normalized_rows, axis=(0, 1)),
            jnp.sum(scaled_product_gradient, axis=(0, 1)),
        ]
    )
    gain_applied = scaled_product_gradient * layer_norm_gain
    alignment_gradient = inverse_deviation * (
        gain_applied
        - jnp.mean(gain_applied, axis=-1, keepdims=True)
        - normalized_rows * jnp.mean(gain_applied * normalized_rows, axis=-1, keepdims=True)
    )
    running_totals = lax.psum((weight_acc, proj_local, bias_local, norm_local), ("wide", "narrow"))
    return (
        alignment_gradient.astype(jnp.bfloat16),
        running_totals[1],
        running_totals[2],
        running_totals[0],
        running_totals[3],
    )


def solution(mesh):
    return jax.shard_map(
        shards,
        mesh=mesh,
        in_specs=(P("wide", "narrow", None), P("wide", "narrow", None), P(), P(), P(), P(), P()),
        out_specs=(P("wide", "narrow", None), P(), P(), P(), P()),
        check_vma=False,
    )
```

profile of v0, /device:TPU:1, one launch (start us, length us, event | category | flops | bytes accessed | tf_op | source)
XLA Modules:
  0.0 440.0 jit_solution(8454498814869465053)
XLA Ops:
  7.2 1.0 convert_reduce_fusion.1
  8.2 1.0 fusion.60
  9.2 1.1 fusion.26
  10.4 0.8 reshape.120
  11.2 10.1 %all-to-all-start.3 = ((bf16[8,2,2048]{2,1,0:T(2,128)(2,1)}), bf16[8,2,2048]{2,1,0:T(2,128)(2,1)S(1)}, u32[]{:S(2)}, u32[]{:S(2)}) async-start(bf16[8,2,2048]{2,1,0:T(2,128)(2,1)} %reshape.120), calls=%async_computation.3 | async-start | bytes 131072 | tf_op jit(solution)/shard_map/all_to_all | solution.py:19
  21.5 1.5 reshape.126
  23.0 5.7 %all-to-all-done.3 = bf16[8,2,2048]{2,1,0:T(2,128)(2,1)S(1)} async-done(((bf16[8,2,2048]{2,1,0:T(2,128)(2,1)}), bf16[8,2,2048]{2,1,0:T(2,128)(2,1)S(1)}, u32[]{:S(2)}, u32[]{:S(2)}) %all-to-all-start.3) | async-done | bytes 65568 | tf_op jit(solution)/shard_map/all_to_all | solution.py:19
  28.7 0.6 copy-done.8
  29.3 12.0 %all-to-all-start = ((bf16[64,2,2048]{2,1,0:T(2,128)(2,1)}), bf16[64,2,2048]{2,1,0:T(2,128)(2,1)S(1)}, u32[]{:S(2)}, u32[]{:S(2)}) async-start(bf16[64,2,2048]{2,1,0:T(2,128)(2,1)} %reshape.126), calls=%async_computation | async-start | bytes 1048576 | tf_op jit(solution)/shard_map/all_to_all | solution.py:19
  43.8 1.1 reshape.84
  45.2 0.8 reshape.122
  46.0 12.9 %all-to-all-done = bf16[64,2,2048]{2,1,0:T(2,128)(2,1)S(1)} async-done(((bf16[64,2,2048]{2,1,0:T(2,128)(2,1)}), bf16[64,2,2048]{2,1,0:T(2,128)(2,1)S(1)}, u32[]{:S(2)}, u32[]{:S(2)}) %all-to-all-start) | async-done | bytes 524320 | tf_op jit(solution)/shard_map/all_to_all | solution.py:19
  59.0 6.1 %all-to-all-start.4 = ((bf16[64,2,256]{2,1,0:T(2,128)(2,1)}), bf16[64,2,256]{2,1,0:T(2,128)(2,1)}, u32[]{:S(2)}, u32[]{:S(2)}) async-start(bf16[64,2,256]{2,1,0:T(2,128)(2,1)} %reshape.122), calls=%async_computation.4 | async-start | bytes 131072 | tf_op jit(solution)/shard_map/all_to_all | solution.py:69
  65.1 0.7 reshape.127
  65.8 1.9 copy.58
  67.7 1.6 fusion.35
  69.3 1.5 fusion.36
  70.8 0.5 fusion.37
  71.3 0.5 fusion.38
  71.8 0.6 pad_maximum_fusion
  72.4 1.7 copy.69
  74.2 1.8 reshape.128
  76.0 11.1 %all-to-all-start.1 = ((bf16[64,2,256]{2,1,0:T(2,128)(2,1)}), bf16[64,2,256]{2,1,0:T(2,128)(2,1)}, u32[]{:S(2)}, u32[]{:S(2)}) async-start(bf16[64,2,256]{2,1,0:T(2,128)(2,1)} %reshape.128), calls=%async_computation.1 | async-start | bytes 131072 | tf_op jit(solution)/shard_map/all_to_all | solution.py:110
  87.1 1.4 copy.78
  88.5 1.4 copy.79
  89.9 1.4 copy.80
  91.3 1.4 copy.81
  92.7 1.1 reshape.123
  94.0 0.8 copy.82
  94.8 1.3 all-to-all-done.1
  96.1 1.1 reshape.129
  97.4 0.8 reshape.130
  98.2 7.3 %all-to-all-start.2 = ((bf16[8,2,2048]{2,1,0:T(2,128)(2,1)}), bf16[8,2,2048]{2,1,0:T(2,128)(2,1)}, u32[]{:S(2)}, u32[]{:S(2)}) async-start(bf16[8,2,2048]{2,1,0:T(2,128)(2,1)} %reshape.130), calls=%async_computation.2 | async-start | bytes 131072 | tf_op jit(solution)/shard_map/all_to_all | solution.py:40
  105.4 2.9 fusion.14
  108.3 3.1 copy.83
  111.4 2.3 reshape.124
  113.7 1.1 copy.103
  114.8 8.3 %all-to-all-start.5 = ((f32[64,1,4096]{2,1,0:T(1,128)}), f32[64,1,4096]{2,1,0:T(1,128)S(1)}, u32[]{:S(2)}, u32[]{:S(2)}) async-start(f32[64,1,4096]{2,1,0:T(1,128)} %reshape.124), calls=%async_computation.5 | async-start | bytes 2097152 | tf_op jit(solution)/shard_map/all_to_all | solution.py:34
  123.1 0.3 all-reduce.4.cloned.1.call-start
  123.3 0.6 fusion.24
  124.0 0.6 copy.86
  124.5 0.2 reshape.94
  124.8 0.6 fusion.23
  125.4 0.6 copy.89
  126.0 0.2 reshape.95
  126.2 0.6 fusion.22
  126.9 0.6 copy.92
  127.4 0.2 reshape.96
  127.7 0.6 fusion.21
  128.3 0.6 copy.95
  129.8 1.0 convolution_add_fusion
  130.8 1.0 reshape.131
  131.8 20.3 %all-to-all-done.5 = f32[64,1,4096]{2,1,0:T(1,128)S(1)} async-done(((f32[64,1,4096]{2,1,0:T(1,128)}), f32[64,1,4096]{2,1,0:T(1,128)S(1)}, u32[]{:S(2)}, u32[]{:S(2)}) %all-to-all-start.5) | async-done | bytes 1048608 | tf_op jit(solution)/shard_map/all_to_all | solution.py:34
  152.1 0.5 broadcast.78
  152.6 3.3 reduce
  155.9 0.8 reshape.125
  156.9 0.5 copy-done.12
  157.5 0.3 fusion.59
  157.9 0.9 convolution_bitcast_fusion.1
  158.8 98.8 %all-reduce = (f32[2,32]{1,0:T(2,128)}, f32[2,256]{1,0:T(2,128)}) all-reduce(f32[2,32]{1,0:T(2,128)S(1)} %fusion.63, f32[2,256]{1,0:T(2,128)S(1)} %pad_maximum_fusion.2), channel_id=1, replica_groups=mesh['wide'=64,'narrow'=8] {'wide','narrow'}, use_global_device_ids=true, to_apply=%region_8.0 | all-reduce | flops 576 | bytes 4608 | tf_op jit(solution)/shard_map/psum | solution.py:135
  257.6 0.8 fusion.58
  258.4 171.4 %all-reduce.4.cloned.1.call-done = (f32[2,256,32]{1,2,0:T(8,128)}, f32[1024,128]{1,0:T(8,128)}) async-done(((f32[2,256,32]{1,2,0:T(8,128)}, f32[1024,128]{1,0:T(8,128)}), (f32[2,256,32]{1,2,0:T(8,128)}, f32[1024,128]{1,0:T(8,128)})) %all-reduce.4.cloned.1.call-update) | async-done | bytes 589840 | tf_op jit(solution)/shard_map/psum | solution.py:135
  429.8 1.5 copy.130
  431.3 1.9 copy.131
  (61 shorter events, 4.5 us)
Async XLA Ops:
  7.2 34.2 %copy-start = (bf16[1024,128]{1,0:T(8,128)(2,1)S(1)}, bf16[1024,128]{1,0:T(8,128)(2,1)}, u32[]{:S(2)}) copy-start(bf16[1024,128]{1,0:T(8,128)(2,1)} %param.13) | copy-start | bytes 786436
  10.3 31.0 %copy-start.10 = (bf16[8,64,128]{2,1,0:T(8,128)(2,1)S(1)}, bf16[8,64,128]{2,1,0:T(8,128)(2,1)}, u32[]{:S(2)}) copy-start(bf16[8,64,128]{2,1,0:T(8,128)(2,1)} %param.8) | copy-start | bytes 393220
  11.2 17.5 %all-to-all-start.3 = ((bf16[8,2,2048]{2,1,0:T(2,128)(2,1)}), bf16[8,2,2048]{2,1,0:T(2,128)(2,1)S(1)}, u32[]{:S(2)}, u32[]{:S(2)}) async-start(bf16[8,2,2048]{2,1,0:T(2,128)(2,1)} %reshape.120), calls=%async_computation.3 | async-start | bytes 131072 | tf_op jit(solution)/shard_map/all_to_all | solution.py:19
  28.7 0.6 copy-start.8
  29.3 29.6 %all-to-all-start = ((bf16[64,2,2048]{2,1,0:T(2,128)(2,1)}), bf16[64,2,2048]{2,1,0:T(2,128)(2,1)S(1)}, u32[]{:S(2)}, u32[]{:S(2)}) async-start(bf16[64,2,2048]{2,1,0:T(2,128)(2,1)} %reshape.126), calls=%async_computation | async-start | bytes 1048576 | tf_op jit(solution)/shard_map/all_to_all | solution.py:19
  42.5 2.4 copy-start.9
  59.0 17.0 %all-to-all-start.4 = ((bf16[64,2,256]{2,1,0:T(2,128)(2,1)}), bf16[64,2,256]{2,1,0:T(2,128)(2,1)}, u32[]{:S(2)}, u32[]{:S(2)}) async-start(bf16[64,2,256]{2,1,0:T(2,128)(2,1)} %reshape.122), calls=%async_computation.4 | async-start | bytes 131072 | tf_op jit(solution)/shard_map/all_to_all | solution.py:69
  65.8 5.5 %copy-start.1 = (bf16[2,64,32,32]{1,0,3,2:T(2,128)(2,1)S(1)}, bf16[2,64,32,32]{1,0,3,2:T(2,128)(2,1)}, u32[]{:S(2)}) copy-start(bf16[2,64,32,32]{1,0,3,2:T(2,128)(2,1)} %reshape.84) | copy-start | bytes 786436
  67.7 3.1 copy-start.3
  76.0 20.2 %all-to-all-start.1 = ((bf16[64,2,256]{2,1,0:T(2,128)(2,1)}), bf16[64,2,256]{2,1,0:T(2,128)(2,1)}, u32[]{:S(2)}, u32[]{:S(2)}) async-start(bf16[64,2,256]{2,1,0:T(2,128)(2,1)} %reshape.128), calls=%async_computation.1 | async-start | bytes 131072 | tf_op jit(solution)/shard_map/all_to_all | solution.py:110
  91.3 14.1 %copy-start.4 = (bf16[2,64,32,32]{1,2,0,3:T(8,128)(2,1)S(1)}, bf16[2,64,32,32]{1,2,0,3:T(8,128)(2,1)}, u32[]{:S(2)}) copy-start(bf16[2,64,32,32]{1,2,0,3:T(8,128)(2,1)} %copy.78) | copy-start | bytes 786436
  91.3 14.1 %copy-start.5 = (bf16[2,64,32,32]{1,2,0,3:T(8,128)(2,1)S(1)}, bf16[2,64,32,32]{1,2,0,3:T(8,128)(2,1)}, u32[]{:S(2)}) copy-start(bf16[2,64,32,32]{1,2,0,3:T(8,128)(2,1)} %copy.79) | copy-start | bytes 786436
  92.7 12.7 %copy-start.6 = (bf16[2,64,32,32]{1,2,0,3:T(8,128)(2,1)S(1)}, bf16[2,64,32,32]{1,2,0,3:T(8,128)(2,1)}, u32[]{:S(2)}) copy-start(bf16[2,64,32,32]{1,2,0,3:T(8,128)(2,1)} %copy.80) | copy-start | bytes 786436
  98.2 16.6 %all-to-all-start.2 = ((bf16[8,2,2048]{2,1,0:T(2,128)(2,1)}), bf16[8,2,2048]{2,1,0:T(2,128)(2,1)}, u32[]{:S(2)}, u32[]{:S(2)}) async-start(bf16[8,2,2048]{2,1,0:T(2,128)(2,1)} %reshape.130), calls=%async_computation.2 | async-start | bytes 131072 | tf_op jit(solution)/shard_map/all_to_all | solution.py:40
  113.7 9.7 %copy-start.7 = (bf16[128,32,8]{0,1,2:T(8,128)(2,1)S(1)}, bf16[128,32,8]{0,1,2:T(8,128)(2,1)}, u32[]{:S(2)}) copy-start(bf16[128,32,8]{0,1,2:T(8,128)(2,1)} %copy.82) | copy-start | bytes 196612
  114.8 37.3 %all-to-all-start.5 = ((f32[64,1,4096]{2,1,0:T(1,128)}), f32[64,1,4096]{2,1,0:T(1,128)S(1)}, u32[]{:S(2)}, u32[]{:S(2)}) async-start(f32[64,1,4096]{2,1,0:T(1,128)} %reshape.124), calls=%async_computation.5 | async-start | bytes 2097152 | tf_op jit(solution)/shard_map/all_to_all | solution.py:34
  123.1 306.7 %all-reduce.4.cloned.1.call-start = ((), (), s32[]{:S(2)}) async-start(), calls=%async_computation.6 | async-start | bytes 1179648 | tf_op jit(solution)/shard_map/psum | solution.py:135
  155.8 1.1 copy-start.2
  155.8 1.1 copy-start.11
  155.9 2.0 copy-start.13
  156.7 0.8 copy-start.12
Sparse Core Ops, SparseCore 0:
  158.9 270.8 all-reduce.3
where the time goes:
time: 441 us; the launch traced here: 440 us
  waiting for transfers between devices  212 us (48%)
  blocking collectives  98.8 us (22%)
  starting transfers between devices  55.2 us (13%)
  local copies, waits for them, and re-layouts  38.5 us (9%)
  between operations  14.6 us (3%)
  matrix products  14.3 us (3%)
  other arithmetic  7 us (2%)
    psum x1, waiting for transfers between devices, shards(): lax.psum((weight_acc, proj_local, bias_local, norm_local), ('wide', 'narr...  171 us
    psum x1, blocking collectives, shards(): lax.psum((weight_acc, proj_local, bias_local, norm_local), ('wide', 'narr...  98.8 us
    all_to_all x2, starting transfers between devices, copy_for_each(): return lax.all_to_all(copies, axis, split_axis=0, concat_axis=0, tiled=True)  22.1 us
    all_to_all x1, waiting for transfers between devices, sum_at_owner(): lax.all_to_all(pieces, axis, split_axis=0, concat_axis=0, tiled=True)  20.3 us
    all_to_all x2, waiting for transfers between devices, copy_for_each(): return lax.all_to_all(copies, axis, split_axis=0, concat_axis=0, tiled=True)  18.6 us
    unnamed x42, local copies, waits for them, and re-layouts  17.4 us
    all_to_all x1, starting transfers between devices, shards(): lax.all_to_all(row_partial.astype(jnp.bfloat16), 'wide', split_axis=0, co...  11.1 us
  transfers between devices with their start and end apart: 7, of which 5 were waited for; matrix products, arithmetic and copies ran while one was open for 10% of the time, Pallas kernels for 0%

commit v1 on v0

--- a/solution.py
+++ b/solution.py
@@ -1,11 +1,18 @@
 import jax
 import jax.numpy as jnp
 from jax import lax
+from jax.experimental import pallas as pl
+from jax.experimental.pallas import tpu as pltpu
 from jax.sharding import PartitionSpec as P
 
 FACTOR_CHANNELS = 32
 PAIR_WIDTH = 128
 OUTER = 1024
+PLANE = 8
+DEPTH = 8
+NARROW = 8
+MESH_ID = pl.DeviceIdType.MESH
+OFFSETS = (4, 3, 5, 2, 6, 1, 7)
 
 
 def in_order(pieces, dim):
@@ -39,6 +46,134 @@
     pieces = in_blocks(array, dim, lax.axis_size(axis))
     arrived = lax.all_to_all(pieces, axis, split_axis=0, concat_axis=0, tiled=True)
     return arrived.astype(jnp.float32).sum(axis=0)
+
+
+def total(ref):
+    acc = ref[0].astype(jnp.float32)
+    for k in range(1, 8):
+        acc = acc + ref[k].astype(jnp.float32)
+    return acc
+
+
+def reduce_kernel(
+    big_ref, small_ref, big_out, small_out,
+    big_send, big_plane, small_plane, big_part, small_part, big_depth, small_depth,
+    big_two, small_two, big_narrow, small_narrow, big_three, small_three, big_gather, big_half,
+    send_sem, recv_sem,
+):
+    wide = lax.axis_index("wide")
+    narrow = lax.axis_index("narrow")
+    plane = wide // DEPTH
+    depth = wide % DEPTH
+    barrier = pltpu.get_barrier_semaphore()
+
+    def peer(kind, k):
+        if kind == "plane":
+            return (k * DEPTH + depth, narrow)
+        if kind == "depth":
+            return (plane * DEPTH + k, narrow)
+        return (wide, k)
+
+    place = {"plane": plane, "depth": depth, "narrow": narrow}
+
+    for kind in ("plane", "depth", "narrow"):
+        for d in OFFSETS:
+            k = (place[kind] + d) % 8
+            pl.semaphore_signal(barrier, 1, device_id=peer(kind, k), device_id_type=MESH_ID)
+    big_send[...] = big_ref[...].astype(jnp.bfloat16).reshape(8, 128, 128)
+    pl.semaphore_wait(barrier, 21)
+
+    def copies(stage, kind, source, target):
+        me = place[kind]
+        made = []
+        for d in OFFSETS:
+            k = (me + d) % 8
+            made.append(
+                pltpu.make_async_remote_copy(
+                    src_ref=source(k),
+                    dst_ref=target.at[me],
+                    send_sem=send_sem.at[stage, d],
+                    recv_sem=recv_sem.at[stage, d],
+                    device_id=peer(kind, k),
+                    device_id_type=MESH_ID,
+                )
+            )
+        for c in made:
+            c.start()
+        return made
+
+    def finish(made):
+        for c in made:
+            c.wait()
+
+    one = copies(0, "plane", lambda k: big_send.at[k], big_plane)
+    two = copies(1, "plane", lambda k: small_ref.at[k], small_plane)
+    big_plane[plane] = big_send[plane]
+    small_plane[plane] = small_ref[plane]
+    finish(two)
+    small_part[...] = total(small_plane)
+    three = copies(2, "depth", lambda k: small_part, small_depth)
+    small_depth[depth] = small_part[...]
+    finish(one)
+    big_part[...] = total(big_plane).reshape(8, 16, 128)
+    four = copies(3, "depth", lambda k: big_part.at[k], big_depth)
+    big_depth[depth] = big_part[depth]
+    finish(three)
+    small_two[...] = total(small_depth)
+    five = copies(4, "narrow", lambda k: small_two, small_narrow)
+    small_narrow[narrow] = small_two[...]
+    finish(four)
+    big_two[...] = total(big_depth)
+    six = copies(5, "narrow", lambda k: big_two, big_narrow)
+    big_narrow[narrow] = big_two[...]
+    finish(five)
+    small_three[...] = total(small_narrow)
+    seven = copies(6, "plane", lambda k: small_three, small_out)
+    small_out[plane] = small_three[...]
+    finish(six)
+    big_three[...] = total(big_narrow)
+    eight = copies(7, "depth", lambda k: big_three, big_gather)
+    big_gather[depth] = big_three[...]
+    finish(eight)
+    big_half[...] = big_gather[...].astype(jnp.bfloat16).reshape(128, 128)
+    nine = copies(8, "plane", lambda k: big_half, big_out)
+    big_out[plane] = big_half[...]
+    finish(seven)
+    finish(nine)
+
+
+def all_sums(big, small):
+    vmem = pl.BlockSpec(memory_space=pltpu.VMEM)
+    f32, b16 = jnp.float32, jnp.bfloat16
+    return pl.pallas_call(
+        reduce_kernel,
+        out_shape=(
+            jax.ShapeDtypeStruct((8, 128, 128), b16),
+            jax.ShapeDtypeStruct((8, 24, 128), f32),
+        ),
+        in_specs=[vmem, vmem],
+        out_specs=(vmem, vmem),
+        scratch_shapes=[
+            pltpu.VMEM((8, 128, 128), b16),
+            pltpu.VMEM((8, 128, 128), b16),
+            pltpu.VMEM((8, 24, 128), f32),
+            pltpu.VMEM((8, 16, 128), f32),
+            pltpu.VMEM((24, 128), f32),
+            pltpu.VMEM((8, 16, 128), f32),
+            pltpu.VMEM((8, 24, 128), f32),
+            pltpu.VMEM((16, 128), f32),
+            pltpu.VMEM((24, 128), f32),
+            pltpu.VMEM((8, 16, 128), f32),
+            pltpu.VMEM((8, 24, 128), f32),
+            pltpu.VMEM((16, 128), f32),
+            pltpu.VMEM((24, 128), f32),
+            pltpu.VMEM((8, 16, 128), f32),
+            pltpu.VMEM((128, 128), b16),
+            pltpu.SemaphoreType.DMA((9, 8)),
+            pltpu.SemaphoreType.DMA((9, 8)),
+        ],
+        compiler_params=pltpu.CompilerParams(collective_id=0, has_side_effects=True),
+    )(big, small)
 
 
 def shards(
@@ -117,7 +252,7 @@
         "kshr,kch->src", factor_grad_b, projection_weight, preferred_element_type=jnp.float32
     )
     proj_local = jnp.einsum(
-        "src,kshr->kch", scaled_product, factor_grad_b, preferred_element_type=jnp.float32
+        "src,kshr->khc", scaled_product, factor_grad_b, preferred_element_type=jnp.float32
     )
     bias_local = jnp.sum(factor_grad, axis=(1, 3))
     norm_local = jnp.stack(
@@ -132,13 +267,22 @@
         - jnp.mean(gain_applied, axis=-1, keepdims=True)
         - normalized_rows * jnp.mean(gain_applied * normalized_rows, axis=-1, keepdims=True)
     )
-    running_totals = lax.psum((weight_acc, proj_local, bias_local, norm_local), ("wide", "narrow"))
+    small = jnp.concatenate(
+        [
+            proj_local.reshape(128, 128),
+            norm_local.reshape(4, 128),
+            jnp.pad(bias_local.reshape(1, 64), ((0, 59), (0, 64))),
+        ]
+    ).reshape(8, 24, 128)
+    big_sum, small_sum = all_sums(weight_acc, small)
+    small_sum = small_sum.reshape(192, 128)
+    proj = small_sum[:128].reshape(2, FACTOR_CHANNELS, 256)
     return (
         alignment_gradient.astype(jnp.bfloat16),
-        running_totals[1],
-        running_totals[2],
-        running_totals[0],
-        running_totals[3],
+        jnp.transpose(proj, (0, 2, 1)),
+        small_sum[132, :64].reshape(2, FACTOR_CHANNELS),
+        big_sum.reshape(OUTER, PAIR_WIDTH).astype(jnp.float32),
+        small_sum[128:132].reshape(2, 256),
     )
 
 

time: 441 us -> 196 us (0.44)
  waiting for transfers between devices: 212 us -> 40.3 us
  blocking collectives: 98.8 us -> 0 us
  Pallas kernels: 0 us -> 35.8 us
  between operations: 14.6 us -> 1.18 us
    psum x1 -> x0, waiting for transfers between devices: 171 us -> none  [shards(): lax.psum((weight_acc, proj_local, bias_local, norm_local), ('wide', 'narr...]
    psum x1 -> x0, blocking collectives: 98.8 us -> none  [shards(): lax.psum((weight_acc, proj_local, bias_local, norm_local), ('wide', 'narr...]
    pallas_call x0 -> x1, Pallas kernels: none -> 35.8 us  [all_sums(): pl.pallas_call(reduce_kernel, out_shape=(jax.ShapeDtypeStruct((8, 128, 12...]
    unnamed x42 -> x40, local copies, waits for them, and re-layouts: 17.4 us -> 14.1 us
  transfers between devices with their start and end apart: 7 -> 6, of which waited for: 5 -> 4; matrix products, arithmetic and copies ran while one was open for 10% -> 22% of each run, Pallas kernels for 0% -> 0%
where the time goes in v1:
time: 196 us; the launch traced here: 195 us
  starting transfers between devices  55.1 us (28%)
  waiting for transfers between devices  40.3 us (21%)
  local copies, waits for them, and re-layouts  39.4 us (20%)
  Pallas kernels  35.8 us (18%)
  matrix products  13.6 us (7%)
  other arithmetic  9.43 us (5%)
    pallas_call x1, Pallas kernels, all_sums(): pl.pallas_call(reduce_kernel, out_shape=(jax.ShapeDtypeStruct((8, 128, 12...  35.8 us
    all_to_all x2, starting transfers between devices, copy_for_each(): return lax.all_to_all(copies, axis, split_axis=0, concat_axis=0, tiled=True)  22.1 us
    all_to_all x1, waiting for transfers between devices, sum_at_owner(): lax.all_to_all(pieces, axis, split_axis=0, concat_axis=0, tiled=True)  20.3 us
    all_to_all x2, waiting for transfers between devices, copy_for_each(): return lax.all_to_all(copies, axis, split_axis=0, concat_axis=0, tiled=True)  18.6 us
    unnamed x40, local copies, waits for them, and re-layouts  14.1 us
    all_to_all x1, starting transfers between devices, shards(): lax.all_to_all(row_partial.astype(jnp.bfloat16), 'wide', split_axis=0, co...  11.1 us
    all_to_all x1, starting transfers between devices, sum_at_owner(): lax.all_to_all(pieces, axis, split_axis=0, concat_axis=0, tiled=True)  8.5 us
    reshape x8, local copies, waits for them, and re-layouts, shards(): upstream.astype(jnp.bfloat16)  7.45 us
  transfers between devices with their start and end apart: 6, of which 4 were waited for; matrix products, arithmetic and copies ran while one was open for 22% of the time, Pallas kernels for 0%

profile of v1, /device:TPU:1, one launch (start us, length us, event | category | flops | bytes accessed | tf_op | source)
XLA Modules:
  0.0 194.8 jit_solution(10323200883867302248)
XLA Ops:
  0.6 1.0 convert_reduce_fusion.1
  1.6 1.0 fusion.60
  2.7 1.1 fusion.26
  3.8 0.8 reshape.159
  4.6 10.1 %all-to-all-start.3 = ((bf16[8,2,2048]{2,1,0:T(2,128)(2,1)}), bf16[8,2,2048]{2,1,0:T(2,128)(2,1)S(1)}, u32[]{:S(2)}, u32[]{:S(2)}) async-start(bf16[8,2,2048]{2,1,0:T(2,128)(2,1)} %reshape.159), calls=%async_computation.3 | async-start | bytes 131072 | tf_op jit(solution)/shard_map/all_to_all | solution.py:26
  15.0 1.5 reshape.165
  16.5 5.7 %all-to-all-done.3 = bf16[8,2,2048]{2,1,0:T(2,128)(2,1)S(1)} async-done(((bf16[8,2,2048]{2,1,0:T(2,128)(2,1)}), bf16[8,2,2048]{2,1,0:T(2,128)(2,1)S(1)}, u32[]{:S(2)}, u32[]{:S(2)}) %all-to-all-start.3) | async-done | bytes 65568 | tf_op jit(solution)/shard_map/all_to_all | solution.py:26
  22.2 0.6 copy-done.8
  22.8 12.0 %all-to-all-start = ((bf16[64,2,2048]{2,1,0:T(2,128)(2,1)}), bf16[64,2,2048]{2,1,0:T(2,128)(2,1)S(1)}, u32[]{:S(2)}, u32[]{:S(2)}) async-start(bf16[64,2,2048]{2,1,0:T(2,128)(2,1)} %reshape.165), calls=%async_computation | async-start | bytes 1048576 | tf_op jit(solution)/shard_map/all_to_all | solution.py:26
  37.3 1.1 reshape.108
  38.7 0.8 reshape.161
  39.5 12.9 %all-to-all-done = bf16[64,2,2048]{2,1,0:T(2,128)(2,1)S(1)} async-done(((bf16[64,2,2048]{2,1,0:T(2,128)(2,1)}), bf16[64,2,2048]{2,1,0:T(2,128)(2,1)S(1)}, u32[]{:S(2)}, u32[]{:S(2)}) %all-to-all-start) | async-done | bytes 524320 | tf_op jit(solution)/shard_map/all_to_all | solution.py:26
  52.5 6.1 %all-to-all-start.4 = ((bf16[64,2,256]{2,1,0:T(2,128)(2,1)}), bf16[64,2,256]{2,1,0:T(2,128)(2,1)}, u32[]{:S(2)}, u32[]{:S(2)}) async-start(bf16[64,2,256]{2,1,0:T(2,128)(2,1)} %reshape.161), calls=%async_computation.4 | async-start | bytes 131072 | tf_op jit(solution)/shard_map/all_to_all | solution.py:204
  58.6 0.7 reshape.166
  59.3 1.9 copy.58
  61.2 1.6 fusion.35
  62.8 1.5 fusion.36
  64.3 0.5 fusion.37
  64.8 0.5 fusion.38
  65.3 0.6 pad_maximum_fusion
  65.9 1.7 copy.69
  67.6 1.8 reshape.167
  69.4 11.1 %all-to-all-start.1 = ((bf16[64,2,256]{2,1,0:T(2,128)(2,1)}), bf16[64,2,256]{2,1,0:T(2,128)(2,1)}, u32[]{:S(2)}, u32[]{:S(2)}) async-start(bf16[64,2,256]{2,1,0:T(2,128)(2,1)} %reshape.167), calls=%async_computation.1 | async-start | bytes 131072 | tf_op jit(solution)/shard_map/all_to_all | solution.py:245
  80.6 1.4 copy.78
  82.0 1.4 copy.79
  83.4 1.4 copy.80
  84.8 1.4 copy.81
  86.2 1.1 reshape.162
  87.5 0.8 copy.82
  88.3 1.4 all-to-all-done.1
  89.6 1.1 reshape.168
  90.9 0.8 reshape.169
  91.7 7.2 %all-to-all-start.2 = ((bf16[8,2,2048]{2,1,0:T(2,128)(2,1)}), bf16[8,2,2048]{2,1,0:T(2,128)(2,1)}, u32[]{:S(2)}, u32[]{:S(2)}) async-start(bf16[8,2,2048]{2,1,0:T(2,128)(2,1)} %reshape.169), calls=%async_computation.2 | async-start | bytes 131072 | tf_op jit(solution)/shard_map/all_to_all | solution.py:47
  98.9 2.9 %fusion.14 = f32[128,32,64]{0,2,1:T(8,128)} fusion(bf16[2,64,32,32]{1,2,0,3:T(8,128)(2,1)} %copy.81, bf16[2,64,32,32]{1,2,0,3:T(8,128)(2,1)S(1)} %copy-done.6, bf16[2,64,32,32]{1,2,0,3:T(8,128)(2,1)S(1)} %copy-done.5, bf16[2,64,32,32]{1,2,0,3:T(8,128)(2,1)S(1)} %copy-done.4, bf16[128,32,8]{0,1,2:T(8,128)(2,1)} %copy.82), kind=kOutput, calls=%fused_computation.14 | convolution fusion | flops 138674176 | bytes 2162688 | tf_op jit(solution)/shard_map/ijpq,spi->sqj/dot_general | solution.py:240
  101.8 3.1 %copy.83 = f32[128,32,64]{2,1,0:T(8,128)S(1)} copy(f32[128,32,64]{0,2,1:T(8,128)} %fusion.14) | data formatting | bytes 2097152 | tf_op jit(solution)/shard_map/div | solution.py:240
  104.8 2.3 %reshape.163 = f32[64,1,4096]{2,1,0:T(1,128)} reshape(f32[64,2,32,64]{3,2,1,0:T(8,128)S(1)} %bitcast.189) | data formatting | bytes 2097152
  107.1 1.1 copy.103
  108.3 8.5 %all-to-all-start.5 = ((f32[64,1,4096]{2,1,0:T(1,128)}), f32[64,1,4096]{2,1,0:T(1,128)S(1)}, u32[]{:S(2)}, u32[]{:S(2)}) async-start(f32[64,1,4096]{2,1,0:T(1,128)} %reshape.163), calls=%async_computation.5 | async-start | bytes 2097152 | tf_op jit(solution)/shard_map/all_to_all | solution.py:41
  116.8 0.6 fusion.24
  117.4 0.6 copy.86
  118.2 0.6 fusion.23
  118.8 0.6 copy.89
  119.7 0.6 fusion.22
  120.3 0.6 copy.92
  121.1 0.6 fusion.21
  121.7 0.6 copy.95
  123.2 1.0 convolution_add_fusion.big_ref
  124.2 1.0 reshape.170
  125.2 20.3 %all-to-all-done.5 = f32[64,1,4096]{2,1,0:T(1,128)S(1)} async-done(((f32[64,1,4096]{2,1,0:T(1,128)}), f32[64,1,4096]{2,1,0:T(1,128)S(1)}, u32[]{:S(2)}, u32[]{:S(2)}) %all-to-all-start.5) | async-done | bytes 1048608 | tf_op jit(solution)/shard_map/all_to_all | solution.py:41
  145.5 0.5 broadcast.87
  146.0 3.3 %reduce.4 = f32[64,4096]{1,0:T(8,128)S(1)} reduce(f32[64,1,4096]{2,1,0:T(1,128)S(1)} %all-to-all-done.5, f32[]{:T(128)} %broadcast.87), dimensions={1}, to_apply=%all_to_all.46.reduce_sub_computation | reduce | bytes 2097156 | tf_op jit(solution)/shard_map/all_to_all | solution.py:41
  149.3 0.8 reshape.164
  150.4 0.5 copy-done.12
  150.9 0.3 fusion.59
  151.7 0.7 select_maximum_fusion
  152.3 35.8 %shard_map.110 = (bf16[8,128,128]{2,1,0:T(8,128)(2,1)}, f32[8,24,128]{2,1,0:T(8,128)}) custom-call(f32[1024,128]{1,0:T(8,128)} %convolution_add_fusion.big_ref, f32[8,24,128]{2,1,0:T(8,128)} %bitcast.198), custom_call_target="tpu_custom_call" | custom-call | tf_op jit(solution)/shard_map/pallas_call | solution.py:148
  188.1 0.8 slice.58
  189.0 0.7 slice.60
  189.7 0.7 slice_reduce_fusion
  190.4 1.8 bitcast_convert_fusion
  192.1 0.6 reshape.127
  192.8 0.6 reshape.128
  193.4 0.6 reshape_squeeze.3
  194.0 0.8 fusion.58
  (67 shorter events, 5.5 us)
Async XLA Ops:
  0.6 34.2 %copy-start = (bf16[1024,128]{1,0:T(8,128)(2,1)S(1)}, bf16[1024,128]{1,0:T(8,128)(2,1)}, u32[]{:S(2)}) copy-start(bf16[1024,128]{1,0:T(8,128)(2,1)} %param.13) | copy-start | bytes 786436
  3.8 31.0 %copy-start.10 = (bf16[8,64,128]{2,1,0:T(8,128)(2,1)S(1)}, bf16[8,64,128]{2,1,0:T(8,128)(2,1)}, u32[]{:S(2)}) copy-start(bf16[8,64,128]{2,1,0:T(8,128)(2,1)} %param.8) | copy-start | bytes 393220
  4.6 17.5 %all-to-all-start.3 = ((bf16[8,2,2048]{2,1,0:T(2,128)(2,1)}), bf16[8,2,2048]{2,1,0:T(2,128)(2,1)S(1)}, u32[]{:S(2)}, u32[]{:S(2)}) async-start(bf16[8,2,2048]{2,1,0:T(2,128)(2,1)} %reshape.159), calls=%async_computation.3 | async-start | bytes 131072 | tf_op jit(solution)/shard_map/all_to_all | solution.py:26
  22.2 0.6 copy-start.8
  22.8 29.6 %all-to-all-start = ((bf16[64,2,2048]{2,1,0:T(2,128)(2,1)}), bf16[64,2,2048]{2,1,0:T(2,128)(2,1)S(1)}, u32[]{:S(2)}, u32[]{:S(2)}) async-start(bf16[64,2,2048]{2,1,0:T(2,128)(2,1)} %reshape.165), calls=%async_computation | async-start | bytes 1048576 | tf_op jit(solution)/shard_map/all_to_all | solution.py:26
  36.0 2.4 %copy-start.9 = (bf16[8,2,2048]{2,1,0:T(2,128)(2,1)S(1)}, bf16[8,2,2048]{2,1,0:T(2,128)(2,1)}, u32[]{:S(2)}) copy-start(bf16[8,2,2048]{2,1,0:T(2,128)(2,1)} %copy-done.8) | copy-start | bytes 196612
  52.5 17.0 %all-to-all-start.4 = ((bf16[64,2,256]{2,1,0:T(2,128)(2,1)}), bf16[64,2,256]{2,1,0:T(2,128)(2,1)}, u32[]{:S(2)}, u32[]{:S(2)}) async-start(bf16[64,2,256]{2,1,0:T(2,128)(2,1)} %reshape.161), calls=%async_computation.4 | async-start | bytes 131072 | tf_op jit(solution)/shard_map/all_to_all | solution.py:204
  59.3 5.5 %copy-start.1 = (bf16[2,64,32,32]{1,0,3,2:T(2,128)(2,1)S(1)}, bf16[2,64,32,32]{1,0,3,2:T(2,128)(2,1)}, u32[]{:S(2)}) copy-start(bf16[2,64,32,32]{1,0,3,2:T(2,128)(2,1)} %reshape.108) | copy-start | bytes 786436
  61.2 3.1 %copy-start.3 = (bf16[128,32,64]{0,2,1:T(8,128)(2,1)S(1)}, bf16[128,32,64]{0,2,1:T(8,128)(2,1)}, u32[]{:S(2)}) copy-start(bf16[128,32,64]{0,2,1:T(8,128)(2,1)} %copy.58) | copy-start | bytes 1572868
  69.4 20.2 %all-to-all-start.1 = ((bf16[64,2,256]{2,1,0:T(2,128)(2,1)}), bf16[64,2,256]{2,1,0:T(2,128)(2,1)}, u32[]{:S(2)}, u32[]{:S(2)}) async-start(bf16[64,2,256]{2,1,0:T(2,128)(2,1)} %reshape.167), calls=%async_computation.1 | async-start | bytes 131072 | tf_op jit(solution)/shard_map/all_to_all | solution.py:245
  84.8 14.1 %copy-start.4 = (bf16[2,64,32,32]{1,2,0,3:T(8,128)(2,1)S(1)}, bf16[2,64,32,32]{1,2,0,3:T(8,128)(2,1)}, u32[]{:S(2)}) copy-start(bf16[2,64,32,32]{1,2,0,3:T(8,128)(2,1)} %copy.78) | copy-start | bytes 786436
  84.8 14.1 %copy-start.5 = (bf16[2,64,32,32]{1,2,0,3:T(8,128)(2,1)S(1)}, bf16[2,64,32,32]{1,2,0,3:T(8,128)(2,1)}, u32[]{:S(2)}) copy-start(bf16[2,64,32,32]{1,2,0,3:T(8,128)(2,1)} %copy.79) | copy-start | bytes 786436
  86.2 12.7 %copy-start.6 = (bf16[2,64,32,32]{1,2,0,3:T(8,128)(2,1)S(1)}, bf16[2,64,32,32]{1,2,0,3:T(8,128)(2,1)}, u32[]{:S(2)}) copy-start(bf16[2,64,32,32]{1,2,0,3:T(8,128)(2,1)} %copy.80) | copy-start | bytes 786436
  91.7 16.6 %all-to-all-start.2 = ((bf16[8,2,2048]{2,1,0:T(2,128)(2,1)}), bf16[8,2,2048]{2,1,0:T(2,128)(2,1)}, u32[]{:S(2)}, u32[]{:S(2)}) async-start(bf16[8,2,2048]{2,1,0:T(2,128)(2,1)} %reshape.169), calls=%async_computation.2 | async-start | bytes 131072 | tf_op jit(solution)/shard_map/all_to_all | solution.py:47
  107.1 9.6 %copy-start.7 = (bf16[128,32,8]{0,1,2:T(8,128)(2,1)S(1)}, bf16[128,32,8]{0,1,2:T(8,128)(2,1)}, u32[]{:S(2)}) copy-start(bf16[128,32,8]{0,1,2:T(8,128)(2,1)} %copy.82) | copy-start | bytes 196612
  108.3 37.3 %all-to-all-start.5 = ((f32[64,1,4096]{2,1,0:T(1,128)}), f32[64,1,4096]{2,1,0:T(1,128)S(1)}, u32[]{:S(2)}, u32[]{:S(2)}) async-start(f32[64,1,4096]{2,1,0:T(1,128)} %reshape.163), calls=%async_computation.5 | async-start | bytes 2097152 | tf_op jit(solution)/shard_map/all_to_all | solution.py:41
  149.3 1.1 copy-start.2
  149.3 1.1 copy-start.11
  149.3 1.9 copy-start.13
  150.2 0.8 copy-start.12

commit v2 on v0

v2 whole, which is shorter than its diff:
```python
import jax
import jax.numpy as jnp
from jax import lax
from jax.experimental import pallas as pl
from jax.experimental.pallas import tpu as pltpu
from jax.sharding import PartitionSpec as P

F32, B16 = jnp.float32, jnp.bfloat16
MESH_ID = pl.DeviceIdType.MESH
OFFSETS = (4, 3, 5, 2, 6, 1, 7)
STAGES = 17
SEQUENCES = 128
(
    ROW_DEPTH, COL_DEPTH, ROW_PAIR, COL_PLANE, COLG_PLANE, ROWG_PAIR, BIG_PLANE, ROWG_DEPTH, COLG_DEPTH,
    BIG_DEPTH, SMALL_PLANE, BIG_NARROW, SMALL_DEPTH, BIG_BACK, SMALL_NARROW, BIG_OUT, SMALL_OUT,
) = range(STAGES)


def dot(a, b, dims):
    return lax.dot_general(a, b, ((dims[:1], dims[1:]), ((), ())), preferred_element_type=F32)


def total(ref):
    acc = ref[0].astype(F32)
    for k in range(1, 8):
        acc = acc + ref[k].astype(F32)
    return acc


def lanes(shape):
    return lax.broadcasted_iota(jnp.int32, shape, len(shape) - 1)


def half_swap(x):
    return pltpu.roll(x, 64, 1)


def kernel(
    x_ref, pair_ref, gain_ref, shift_ref, weight_ref, bias_ref, out_weight_ref,
    align_out, proj_out, bias_out, norm_out, big_out,
    normed, scaled, scaled32, inverse, row_tmp,
    row_send, col_send, row_got, col_got, col_wide, row_next, col_next,
    row_pair, col_plane, pair_order, weight32, weight_order, upstream, rows, rows_t, cols, outer,
    colg_send, colg_got, rowg_acc, rowg_send, rowg_got, rowg_next, rowg_depth, rowg,
    colg_wide, colg_next, colg_depth, scaled_grad,
    big_send, big_plane, big_part, big_depth, big_two, big_narrow, big_three, big_back, big_half,
    small_in, small_plane, small_part, small_depth, small_two, small_narrow, small_three, small_all,
    send_sem, recv_sem,
):
    wide = lax.axis_index("wide")
    narrow = lax.axis_index("narrow")
    plane = wide // 8
    depth = wide % 8
    own_pair = plane == narrow
    other_pair = plane != narrow
    barrier = pltpu.get_barrier_semaphore()
    place = {"plane": plane, "depth": depth, "narrow": narrow}

    def peer(kind, k):
        if kind == "plane":
            return (k * 8 + depth, narrow)
        if kind == "depth":
            return (plane * 8 + k, narrow)
        return (wide, k)

    def holder(d):
        return (narrow * 8 + depth, (narrow + d) % 8)

    def source(d):
        return (((plane + d) % 8) * 8 + depth, plane)

    def greet(device):
        pl.semaphore_signal(barrier, 1, device_id=device, device_id_type=MESH_ID)

    for kind in ("plane", "depth", "narrow"):
        for d in OFFSETS:
            greet(peer(kind, (place[kind] + d) % 8))
    for d in range(1, 8):
        greet(holder(d))
        greet(source(d))

    @pl.when(other_pair)
    def _():
        greet(holder(0))
        greet(source(0))

    def copies(stage, kind, give, target):
        me = place[kind]
        made = []
        for d in OFFSETS:
            k = (me + d) % 8
            c = pltpu.make_async_remote_copy(
                src_ref=give(k),
                dst_ref=target(me),
                send_sem=send_sem.at[stage, d],
                recv_sem=recv_sem.at[stage, d],
                device_id=peer(kind, k),
                device_id_type=MESH_ID,
            )
            c.start()
            made.append(c)
        return made

    def finish(made):
        for c in made:
            c.wait()

    def pair_copies(stage, device, tag, give, target, own):
        made = []
        for d in range(8):
            c = pltpu.make_async_remote_copy(
                src_ref=give(d),
                dst_ref=target.at[tag],
                send_sem=send_sem.at[stage, d],
                recv_sem=recv_sem.at[stage, tag],
                device_id=device(d),
                device_id_type=MESH_ID,
            )
            k = (tag + d) % 8
            arrival = pltpu.make_async_remote_copy(
                src_ref=give(d),
                dst_ref=target.at[k],
                send_sem=send_sem.at[stage, d],
                recv_sem=recv_sem.at[stage, k],
                device_id=device(d),
                device_id_type=MESH_ID,
            )
            made.append((c, arrival))
        for c, _ in made[1:]:
            c.start()

        @pl.when(other_pair)
        def _():
            made[0][0].start()

        @pl.when(own_pair)
        def _():
            own()

        return made

    def pair_finish(made):
        for c, arrival in made[1:]:
            c.wait_send()
            arrival.wait_recv()

        @pl.when(other_pair)
        def _():
            made[0][0].wait_send()
            made[0][1].wait_recv()

    value = x_ref[...].astype(F32)
    centre = value - jnp.mean(value, axis=-1, keepdims=True)
    inv = lax.rsqrt(jnp.mean(centre * centre, axis=-1, keepdims=True) + 1e-05)
    norm = centre * inv
    inverse[...] = jnp.broadcast_to(inv, (128, 128))
    normed[...] = norm
    scaled_b = (norm * gain_ref[...] + shift_ref[...]).astype(B16)
    scaled[...] = scaled_b
    for c in range(2):
        scaled32[c] = scaled_b[:, c * 128 : c * 128 + 128].astype(F32)

    def every_fourth(g):
        both = [scaled32[c, pl.ds(g, 32, stride=4), :] for c in range(2)]
        return jnp.concatenate(both, axis=1).astype(B16)

    w_row = weight_ref[0:32, :]
    w_col = weight_ref[32:64, :]
    w_row4 = jnp.concatenate([w_row] * 4, axis=0)
    sub = lax.broadcasted_iota(jnp.int32, (32, 32), 0)
    diagonal = sub == lanes((32, 32))
    row_bias = jnp.sum(jnp.where(diagonal, bias_ref[0:1, :], 0.0), axis=1, keepdims=True)
    col_bias = jnp.sum(jnp.where(diagonal, bias_ref[1:2, :], 0.0), axis=1, keepdims=True)
    lane128 = lanes((32, 128))
    sub128 = lax.broadcasted_iota(jnp.int32, (32, 128), 0)
    row_bias4 = jnp.sum(jnp.where(sub128 == lane128 % 32, row_bias, 0.0), axis=0, keepdims=True)
    group = lane128 // 32
    row_fac = jnp.zeros((32, 128), F32)
    for g in range(4):
        row_fac = jnp.where(group == g, dot(every_fourth(g), w_row4, (1, 1)), row_fac)
    row_tmp[...] = (row_fac + row_bias4).astype(B16).astype(F32)
    row_send[...] = jnp.zeros((64, 128), F32)
    for r in range(2):
        for h in range(2):
            row_send[pl.ds(r * 2 + h, 8, stride=8), :] = row_tmp[pl.ds(r * 16 + h, 8, stride=2), :]
    col_send[...] = (dot(w_col, scaled_b, (1, 1)) + col_bias).astype(B16)
    pl.semaphore_wait(barrier, jnp.where(other_pair, 37, 35))

    def eight(ref, k):
        return ref.at[pl.ds(pl.multiple_of(k * 8, 8), 8)]

    row_depth_c = copies(ROW_DEPTH, "depth", lambda k: eight(row_send, k), lambda m: eight(row_got, m))
    col_depth_c = copies(COL_DEPTH, "depth", lambda k: col_send, lambda m: col_got.at[m])
    mine = pl.ds(pl.multiple_of(depth * 8, 8), 8)
    row_got[mine, :] = row_send[mine, :]
    col_got[depth] = col_send[...]

    for g in range(4):
        for h in range(2):
            i = h * 4 + g
            pair_order[pl.ds(g * 128 + h * 64, 64), :] = pair_ref[pl.ds(i * 64, 64), :]
    weight32[...] = out_weight_ref[...].astype(F32)

    def reorder(q, _):
        weight_order[q] = weight32[pl.ds(q, 32, stride=32), :].astype(B16)
        return 0

    lax.fori_loop(0, 32, reorder, 0)

    def up(b, _):
        w = weight_order[pl.ds(b * 2, 2)].reshape(64, 128)
        res = dot(w, pair_order[...], (1, 1)).astype(B16)
        for t in range(2):
            for g in range(4):
                upstream[b, pl.ds(g * 32, 32), pl.ds(t * 128, 128)] = res[t * 32 : t * 32 + 32, g * 128 : g * 128 + 128]
        return 0

    lax.fori_loop(0, 16, up, 0)

    finish(row_depth_c)
    for h in range(2):
        both = [row_got[pl.ds(r * 2 + h, 8, stride=8), :] for r in range(2)]
        row_next[h] = jnp.concatenate(both, axis=0).astype(B16)

    def keep_row():
        row_pair[plane] = row_next[...]

    row_pair_c = pair_copies(ROW_PAIR, holder, plane, lambda d: row_next, row_pair, keep_row)

    finish(col_depth_c)
    col_wide[...] = col_got[...].astype(F32).reshape(256, 128)
    low8 = lanes((8, 128)) < 64

    def spread(b, _):
        x0 = col_wide[pl.ds(b * 2, 8, stride=32), :]
        x1 = col_wide[pl.ds(b * 2 + 1, 8, stride=32), :]
        r0 = jnp.where(low8, x0, half_swap(x1))
        r1 = jnp.where(low8, half_swap(x0), x1)
        col_next[b] = jnp.concatenate([r0, r1], axis=0).astype(B16)
        return 0

    lax.fori_loop(0, 16, spread, 0)
    col_plane_c = copies(COL_PLANE, "plane", lambda k: col_next, lambda m: col_plane.at[m])
    col_plane[plane] = col_next[...]

    pair_finish(row_pair_c)
    for h in range(2):
        rows[pl.ds(h * 128, 128), :] = row_pair[:, h].reshape(128, 128)
    rows_t[...] = rows[...].astype(F32).T.astype(B16)
    low = lanes((128, 128)) < 64

    def col_grad(b, _):
        r = dot(rows[...], upstream[b], (1, 0))
        a = jnp.where(low, r[:128, :128], r[128:, 128:])
        c = jnp.where(low, r[:128, 128:], r[128:, :128])
        out = (a + half_swap(c)) * (1.0 / SEQUENCES)
        colg_send[:, b] = out.astype(B16).reshape(8, 16, 128)
        return 0

    lax.fori_loop(0, 16, col_grad, 0)
    colg_plane_c = copies(COLG_PLANE, "plane", lambda k: colg_send.at[k], lambda m: colg_got.at[m])
    colg_got[plane] = colg_send[plane]

    finish(col_plane_c)
    rowg_acc[...] = jnp.zeros((128, 256), F32)

    def row_grad(b, _):
        c = col_plane[:, b].reshape(128, 128).astype(F32)
        s = half_swap(c)
        cols[b, pl.ds(0, 128), pl.ds(0, 128)] = jnp.where(low, c, 0.0).astype(B16)
        cols[b, pl.ds(128, 128), pl.ds(0, 128)] = jnp.where(low, 0.0, s).astype(B16)
        cols[b, pl.ds(0, 128), pl.ds(128, 128)] = jnp.where(low, s, 0.0).astype(B16)
        cols[b, pl.ds(128, 128), pl.ds(128, 128)] = jnp.where(low, 0.0, c).astype(B16)
        rowg_acc[...] += dot(upstream[b], cols[b], (1, 1))
        return 0

    lax.fori_loop(0, 16, row_grad, 0)
    grad_t = (rowg_acc[...].T * (1.0 / SEQUENCES)).astype(B16)
    for h in range(2):
        rowg_send[:, h] = grad_t[h * 128 : h * 128 + 128].reshape(8, 16, 128)

    def keep_rowg():
        rowg_got[narrow] = rowg_send[plane]

    rowg_pair_c = pair_copies(
        ROWG_PAIR, source, narrow, lambda d: rowg_send.at[(plane + d) % 8], rowg_got, keep_rowg
    )

    def outer_prod(b, _):
        o = (dot(rows_t[...], cols[b], (1, 0)) * (1.0 / SEQUENCES)).astype(B16)
        for t in range(2):
            for g in range(4):
                outer[b * 2 + t, :, pl.ds(g * 128, 128)] = o[g * 32 : g * 32 + 32, t * 128 : t * 128 + 128]
        return 0

    lax.fori_loop(0, 16, outer_prod, 0)

    def weight_grad(k, _):
        o = outer[pl.ds(k * 4, 4)].reshape(128, 512)
        big_send[k] = dot(o, pair_order[...], (1, 0)).astype(B16)
        return 0

    lax.fori_loop(0, 8, weight_grad, 0)
    big_plane_c = copies(BIG_PLANE, "plane", lambda k: big_send.at[k], lambda m: big_plane.at[m])
    big_plane[plane] = big_send[plane]

    pair_finish(rowg_pair_c)
    row_sum = total(rowg_got)
    rowg_next[...] = jnp.zeros((64, 128), F32)
    for h in range(2):
        for r in range(2):
            rowg_next[pl.ds(r * 2 + h, 8, stride=8), :] = row_sum[h, r * 8 : r * 8 + 8, :]
    rowg_depth_c = copies(ROWG_DEPTH, "depth", lambda k: eight(rowg_next, k), lambda m: eight(rowg_depth, m))
    rowg_depth[mine, :] = rowg_next[mine, :]

    finish(colg_plane_c)

    def collect(b, _):
        acc = colg_got[0, b].astype(F32)
        for k in range(1, 8):
            acc = acc + colg_got[k, b].astype(F32)
        y0, y1 = acc[:8], acc[8:]
        colg_wide[pl.ds(b * 2, 8, stride=32), :] = jnp.where(low8, y0, half_swap(y1))
        colg_wide[pl.ds(b * 2 + 1, 8, stride=32), :] = jnp.where(low8, half_swap(y0), y1)
        return 0

    lax.fori_loop(0, 16, collect, 0)
    colg_next[...] = colg_wide[...].astype(B16).reshape(8, 32, 128)
    colg_depth_c = copies(COLG_DEPTH, "depth", lambda k: colg_next.at[k], lambda m: colg_depth.at[m])
    colg_depth[depth] = colg_next[depth]

    finish(big_plane_c)
    big_part[...] = total(big_plane).reshape(8, 16, 128)
    big_depth_c = copies(BIG_DEPTH, "depth", lambda k: big_part.at[k], lambda m: big_depth.at[m])
    big_depth[depth] = big_part[depth]

    finish(rowg_depth_c)
    for h in range(2):
        for r in range(2):
            rowg[pl.ds(r * 16 + h, 8, stride=2), :] = rowg_depth[pl.ds(r * 2 + h, 8, stride=8), :]
    row_g = rowg[...]
    row_gb = row_g.astype(B16)
    row_fold = jnp.sum(row_g, axis=0, keepdims=True)
    row_fold = row_fold + pltpu.roll(row_fold, 32, 1) + pltpu.roll(row_fold, 64, 1) + pltpu.roll(row_fold, 96, 1)
    finish(colg_depth_c)
    col_g = total(colg_depth)
    col_gb = col_g.astype(B16)
    col_sum = jnp.sum(col_g, axis=1, keepdims=True)
    col_fold = jnp.sum(jnp.where(sub128 == lane128, col_sum, 0.0), axis=0, keepdims=True)
    from_cols = dot(col_gb, w_col, (0, 0))
    for c in range(2):
        scaled_grad[c] = from_cols[:, c * 128 : c * 128 + 128]
    proj_col = dot(col_gb, scaled[...], (1, 0))
    proj_row4 = jnp.zeros((128, 256), F32)
    for g in range(4):
        masked = jnp.where(group == g, row_gb.astype(F32), 0.0).astype(B16)
        more = dot(masked, w_row4, (1, 0))
        for c in range(2):
            spot = (c, pl.ds(g, 32, stride=4), slice(None))
            scaled_grad[spot] = scaled_grad[spot] + more[:, c * 128 : c * 128 + 128]
        proj_row4 = proj_row4 + dot(masked, every_fourth(g), (0, 0))
    proj_row = proj_row4[0:32] + proj_row4[32:64] + proj_row4[64:96] + proj_row4[96:128]
    grad = jnp.concatenate([scaled_grad[0], scaled_grad[1]], axis=1)
    norm = normed[...]
    gain_grad = jnp.sum(grad * norm, axis=0, keepdims=True)
    shift_grad = jnp.sum(grad, axis=0, keepdims=True)
    small_in[pl.ds(0, 32), :] = proj_row[:, :128]
    small_in[pl.ds(32, 32), :] = proj_col[:, :128]
    small_in[pl.ds(64, 32), :] = proj_row[:, 128:]
    small_in[pl.ds(96, 32), :] = proj_col[:, 128:]
    small_in[pl.ds(128, 64), :] = jnp.zeros((64, 128), F32)
    small_in[pl.ds(128, 1), :] = gain_grad[:, :128]
    small_in[pl.ds(129, 1), :] = gain_grad[:, 128:]
    small_in[pl.ds(130, 1), :] = shift_grad[:, :128]
    small_in[pl.ds(131, 1), :] = shift_grad[:, 128:]
    small_in[pl.ds(132, 1), :] = row_fold
    small_in[pl.ds(133, 1), :] = col_fold

    def strip(ref, k):
        return ref.at[pl.ds(pl.multiple_of(k * 24, 8), 24)]

    small_plane_c = copies(SMALL_PLANE, "plane", lambda k: strip(small_in, k), lambda m: small_plane.at[m])
    small_plane[plane] = small_in[pl.ds(pl.multiple_of(plane * 24, 8), 24), :]

    inv = inverse[...][:, :1]
    gained = grad * gain_ref[...]
    align = inv * (
        gained
        - jnp.mean(gained, axis=-1, keepdims=True)
        - norm * jnp.mean(gained * norm, axis=-1, keepdims=True)
    )
    align_out[...] = align.astype(B16)

    finish(big_depth_c)
    big_two[...] = total(big_depth)
    big_narrow_c = copies(BIG_NARROW, "narrow", lambda k: big_two, lambda m: big_narrow.at[m])
    big_narrow[narrow] = big_two[...]

    finish(small_plane_c)
    small_part[...] = total(small_plane)
    small_depth_c = copies(SMALL_DEPTH, "depth", lambda k: small_part, lambda m: small_depth.at[m])
    small_depth[depth] = small_part[...]

    finish(big_narrow_c)
    big_three[...] = total(big_narrow)
    big_back_c = copies(BIG_BACK, "depth", lambda k: big_three, lambda m: big_back.at[m])
    big_back[depth] = big_three[...]

    finish(small_depth_c)
    small_two[...] = total(small_depth)
    small_narrow_c = copies(SMALL_NARROW, "narrow", lambda k: small_two, lambda m: small_narrow.at[m])
    small_narrow[narrow] = small_two[...]

    finish(big_back_c)
    big_half[...] = big_back[...].astype(B16).reshape(128, 128)
    big_out_c = copies(BIG_OUT, "plane", lambda k: big_half, lambda m: big_out.at[m])
    big_out[plane] = big_half[...]

    finish(small_narrow_c)
    small_three[...] = total(small_narrow)
    small_out_c = copies(SMALL_OUT, "plane", lambda k: small_three, lambda m: strip(small_all, m))
    small_all[pl.ds(pl.multiple_of(plane * 24, 8), 24), :] = small_three[...]

    finish(small_out_c)
    proj_out[:, pl.ds(0, 128)] = small_all[pl.ds(0, 64), :]
    proj_out[:, pl.ds(128, 128)] = small_all[pl.ds(64, 64), :]
    norm_out[:, pl.ds(0, 128)] = small_all[pl.ds(128, 2, stride=2), :]
    norm_out[:, pl.ds(128, 128)] = small_all[pl.ds(129, 2, stride=2), :]
    bias_out[...] = small_all[pl.ds(132, 2), pl.ds(0, 32)]
    finish(big_out_c)


def everything(x, pair, gain, shift, weight, bias, out_weight):
    vmem = pl.BlockSpec(memory_space=pltpu.VMEM)
    scratch = [
        ((128, 256), F32), ((128, 256), B16), ((2, 128, 128), F32), ((128, 128), F32), ((32, 128), F32),
        ((64, 128), F32), ((32, 128), B16), ((64, 128), F32), ((8, 32, 128), B16), ((256, 128), F32),
        ((2, 16, 128), B16), ((16, 16, 128), B16),
        ((8, 2, 16, 128), B16), ((8, 16, 16, 128), B16), ((512, 128), B16), ((1024, 128), F32),
        ((32, 32, 128), B16), ((16, 128, 256), B16), ((256, 128), B16), ((128, 256), B16),
        ((16, 256, 256), B16), ((32, 32, 512), B16),
        ((8, 16, 16, 128), B16), ((8, 16, 16, 128), B16), ((128, 256), F32), ((8, 2, 16, 128), B16),
        ((8, 2, 16, 128), B16), ((64, 128), F32), ((64, 128), F32), ((32, 128), F32),
        ((256, 128), F32), ((8, 32, 128), B16), ((8, 32, 128), B16), ((2, 128, 128), F32),
        ((8, 128, 128), B16), ((8, 128, 128), B16), ((8, 16, 128), F32), ((8, 16, 128), F32), ((16, 128), F32),
        ((8, 16, 128), F32), ((16, 128), F32), ((8, 16, 128), F32), ((128, 128), B16),
        ((192, 128), F32), ((8, 24, 128), F32), ((24, 128), F32), ((8, 24, 128), F32), ((24, 128), F32),
        ((8, 24, 128), F32), ((24, 128), F32), ((192, 128), F32),
    ]
    return pl.pallas_call(
        kernel,
        out_shape=(
            jax.ShapeDtypeStruct((128, 256), B16),
            jax.ShapeDtypeStruct((64, 256), F32),
            jax.ShapeDtypeStruct((2, 32), F32),
            jax.ShapeDtypeStruct((2, 256), F32),
            jax.ShapeDtypeStruct((8, 128, 128), B16),
        ),
        in_specs=[vmem] * 7,
        out_specs=(vmem,) * 5,
        scratch_shapes=[pltpu.VMEM(shape, kind) for shape, kind in scratch]
        + [pltpu.SemaphoreType.DMA((STAGES, 8)), pltpu.SemaphoreType.DMA((STAGES, 8))],
        compiler_params=pltpu.CompilerParams(
            collective_id=0, has_side_effects=True, vmem_limit_bytes=56 * 1024 * 1024
        ),
    )(x, pair, gain, shift, weight, bias, out_weight)


def shards(
    alignment_rows,
    pair_output_gradient,
    layer_norm_gain,
    layer_norm_bias,
    projection_weight,
    projection_bias,
    output_weight,
):
    align, proj, bias, norm, big = everything(
        alignment_rows.reshape(128, 256),
        pair_output_gradient.reshape(512, 128),
        layer_norm_gain.reshape(1, 256),
        layer_norm_bias.reshape(1, 256),
        jnp.transpose(projection_weight, (0, 2, 1)).reshape(64, 256),
        projection_bias,
        output_weight,
    )
    weight_grad = jnp.transpose(big.reshape(32, 32, 128), (1, 0, 2)).reshape(1024, 128)
    return (
        align.reshape(2, 64, 256),
        jnp.transpose(proj.reshape(2, 32, 256), (0, 2, 1)),
        bias,
        weight_grad.astype(F32),
        norm,
    )


def solution(mesh):
    return jax.shard_map(
        shards,
        mesh=mesh,
        in_specs=(P("wide", "narrow", None), P("wide", "narrow", None), P(), P(), P(), P(), P()),
        out_specs=(P("wide", "narrow", None), P(), P(), P(), P()),
        check_vma=False,
    )
```

time: 441 us -> 77.4 us (0.18)
  waiting for transfers between devices: 212 us -> 0 us
  blocking collectives: 98.8 us -> 0 us
  Pallas kernels: 0 us -> 71.6 us
  starting transfers between devices: 55.2 us -> 0 us
  local copies, waits for them, and re-layouts: 38.5 us -> 3.88 us
  matrix products: 14.3 us -> 0 us
  between operations: 14.6 us -> 0.66 us
  other arithmetic: 7 us -> 1 us
    psum x1 -> x0, waiting for transfers between devices: 171 us -> none  [shards(): lax.psum((weight_acc, proj_local, bias_local, norm_local), ('wide', 'narr...]
    psum x1 -> x0, blocking collectives: 98.8 us -> none  [shards(): lax.psum((weight_acc, proj_local, bias_local, norm_local), ('wide', 'narr...]
    pallas_call x0 -> x1, Pallas kernels: none -> 71.6 us  [everything(): pl.pallas_call(kernel, out_shape=(jax.ShapeDtypeStruct((128, 256), B16),...]
    all_to_all x6 -> x0, starting transfers between devices: 54.9 us -> none  [the longest x2 22.1 us: copy_for_each(): return lax.all_to_all(copies, axis, split_axis=0, concat_axis=0, tiled=True)]
    all_to_all x6 -> x0, waiting for transfers between devices: 40.2 us -> none  [the longest x1 20.3 us: sum_at_owner(): lax.all_to_all(pieces, axis, split_axis=0, concat_axis=0, tiled=True)]
    unnamed x42 -> x12, local copies, waits for them, and re-layouts: 17.4 us -> 2.78 us
    dot_general x20 -> x0, matrix products: 14.3 us -> none  [the longest x4 4.07 us: shards(): jnp.einsum('ijpq,sqj->spi', upstream, col_whole, preferred_element_type=j...]
    reshape x15 -> x0, local copies, waits for them, and re-layouts: 11.6 us -> none  [the longest x8 7.44 us: shards(): upstream.astype(jnp.bfloat16)]
  transfers between devices with their start and end apart: 7 -> 0, of which waited for: 5 -> 0; matrix products, arithmetic and copies ran while one was open for 10% -> 0% of each run, Pallas kernels for 0% -> 0%
where the time goes in v2:
time: 77.4 us; the launch traced here: 77.1 us
  Pallas kernels  71.6 us (93%)
  local copies, waits for them, and re-layouts  3.88 us (5%)
  other arithmetic  1 us (1%)
    pallas_call x1, Pallas kernels, everything(): pl.pallas_call(kernel, out_shape=(jax.ShapeDtypeStruct((128, 256), B16),...  71.6 us
    unnamed x12, local copies, waits for them, and re-layouts  2.78 us

profile of v2, /device:TPU:1, one launch (start us, length us, event | category | flops | bytes accessed | tf_op | source)
XLA Modules:
  0.0 77.1 jit_solution(16202654622115354151)
XLA Ops:
  0.6 71.6 %shard_map.110 = (bf16[128,256]{1,0:T(8,128)(2,1)}, f32[64,256]{1,0:T(8,128)}, f32[2,32]{1,0:T(2,128)}, f32[2,256]{1,0:T(2,128)}, bf16[8,128,128]{2,1,0:T(8,128)(2,1)}) custom-call(bf16[128,256]{1,0:T(8,128)(2,1)} %bitcast.19, bf16[512,128]{1,0:T(8,128)(2,1)} %bitcast.18, f32[1,256]{1,0:T(1,128)} %bitcast.23, f32[1,256]{1,0:T(1,128)} %bitcast.24, ...), custom_call_target="tpu_custom_call" | custom-call | tf_op jit(solution)/shard_map/pallas_call | solution.py:450
  72.2 1.0 %convert_bitcast_fusion = f32[32,32,128]{2,0,1:T(8,128)S(1)} fusion(bf16[32,32,128]{2,1,0:T(8,128)(2,1)} %bitcast.17), kind=kLoop, calls=%fused_computation | loop fusion | flops 131072 | bytes 786432 | tf_op jit(solution)/shard_map/convert_element_type | solution.py:492
  73.2 0.0 copy-start.1
  73.2 1.1 %copy.12 = f32[32,32,128]{2,1,0:T(8,128)} copy(f32[32,32,128]{2,0,1:T(8,128)S(1)} %convert_bitcast_fusion) | data formatting | bytes 1048576 | tf_op jit(solution)/shard_map/convert_element_type | solution.py:492
  74.3 0.0 copy-done.1
  74.3 0.0 copy-start
  74.3 0.6 copy.17
  75.0 0.2 copy-done
  75.2 0.0 copy-start.3
  75.2 0.6 copy.18
  75.8 0.0 copy-done.3
  75.9 0.0 copy-start.2
  75.9 0.6 copy.19
  76.4 0.1 copy-done.2
  76.5 0.6 copy.20
Async XLA Ops:
  73.2 1.1 %copy-start.1 = (bf16[128,256]{1,0:T(8,128)(2,1)S(1)}, bf16[128,256]{1,0:T(8,128)(2,1)}, u32[]{:S(2)}) copy-start(bf16[128,256]{1,0:T(8,128)(2,1)} %get-tuple-element.10) | copy-start | bytes 196612
  74.3 0.9 %copy-start = (f32[64,256]{1,0:T(8,128)S(1)}, f32[64,256]{1,0:T(8,128)}, u32[]{:S(2)}) copy-start(f32[64,256]{1,0:T(8,128)} %get-tuple-element.11) | copy-start | bytes 196612
  75.2 0.7 copy-start.3
  75.9 0.7 copy-start.2

commit v3 on v2

--- a/solution.py
+++ b/solution.py
@@ -36,16 +36,16 @@
 
 
 def kernel(
-    x_ref, pair_ref, gain_ref, shift_ref, weight_ref, bias_ref, out_weight_ref,
-    align_out, proj_out, bias_out, norm_out, big_out,
+    x_ref, pair_hbm, gain_ref, shift_ref, weight_ref, bias_ref, out_weight_hbm,
+    align_out, proj_out, bias_out, norm_out, weight_out,
     normed, scaled, scaled32, inverse, row_tmp,
     row_send, col_send, row_got, col_got, col_wide, row_next, col_next,
-    row_pair, col_plane, pair_order, weight32, weight_order, upstream, rows, rows_t, cols, outer,
-    colg_send, colg_got, rowg_acc, rowg_send, rowg_got, rowg_next, rowg_depth, rowg,
+    row_pair, col_plane, pair_ref, out_weight_ref, pair_two, weight32, weight_order, upstream, rows, rows_t, outer,
+    colg_send, colg_got, rowg_send, rowg_got, rowg_next, rowg_depth, rowg,
     colg_wide, colg_next, colg_depth, scaled_grad,
-    big_send, big_plane, big_part, big_depth, big_two, big_narrow, big_three, big_back, big_half,
+    big_send, big_plane, big_part, big_depth, big_two, big_narrow, big_three, big_back, big_half, big_all,
     small_in, small_plane, small_part, small_depth, small_two, small_narrow, small_three, small_all,
-    send_sem, recv_sem,
+    send_sem, recv_sem, local_sem,
 ):
     wide = lax.axis_index("wide")
     narrow = lax.axis_index("narrow")
@@ -54,6 +54,10 @@
     own_pair = plane == narrow
     other_pair = plane != narrow
     barrier = pltpu.get_barrier_semaphore()
+    fetch_pair = pltpu.make_async_copy(pair_hbm, pair_ref, local_sem.at[0])
+    fetch_weight = pltpu.make_async_copy(out_weight_hbm, out_weight_ref, local_sem.at[1])
+    fetch_pair.start()
+    fetch_weight.start()
     place = {"plane": plane, "depth": depth, "narrow": narrow}
 
     def peer(kind, k):
@@ -195,27 +199,27 @@
     row_got[mine, :] = row_send[mine, :]
     col_got[depth] = col_send[...]
 
-    for g in range(4):
-        for h in range(2):
-            i = h * 4 + g
-            pair_order[pl.ds(g * 128 + h * 64, 64), :] = pair_ref[pl.ds(i * 64, 64), :]
+    fetch_weight.wait()
     weight32[...] = out_weight_ref[...].astype(F32)
-
-    def reorder(q, _):
-        weight_order[q] = weight32[pl.ds(q, 32, stride=32), :].astype(B16)
+    for q in range(32):
+        weight_order[pl.ds(q * 32, 32), :] = weight32[pl.ds(q, 32, stride=32), :].astype(B16)
+    fetch_pair.wait()
+    low32 = lane128 < 64
+
+    def up(c, _):
+        w = weight_order[pl.ds(pl.multiple_of(c * 256, 256), 256), :]
+        res = dot(w, pair_ref[...], (1, 1))
+        for b in range(4):
+            for i in range(4):
+                even = res[b * 64 : b * 64 + 32, i * 128 : i * 128 + 128]
+                odd = res[b * 64 + 32 : b * 64 + 64, i * 128 : i * 128 + 128]
+                spot = (c * 2 + b // 2, pl.ds(i * 64, 64), pl.ds((b % 2) * 128, 128))
+                first = jnp.where(low32, even, half_swap(odd))
+                second = jnp.where(low32, half_swap(even), odd)
+                upstream[spot] = jnp.concatenate([first, second], axis=0).astype(B16)
         return 0
 
-    lax.fori_loop(0, 32, reorder, 0)
-
-    def up(b, _):
-        w = weight_order[pl.ds(b * 2, 2)].reshape(64, 128)
-        res = dot(w, pair_order[...], (1, 1)).astype(B16)
-        for t in range(2):
-            for g in range(4):
-                upstream[b, pl.ds(g * 32, 32), pl.ds(t * 128, 128)] = res[t * 32 : t * 32 + 32, g * 128 : g * 128 + 128]
-        return 0
-
-    lax.fori_loop(0, 16, up, 0)
+    lax.fori_loop(0, 4, up, 0)
 
     finish(row_depth_c)
     for h in range(2):
@@ -231,53 +235,42 @@
     col_wide[...] = col_got[...].astype(F32).reshape(256, 128)
     low8 = lanes((8, 128)) < 64
 
-    def spread(b, _):
+    for b in range(16):
         x0 = col_wide[pl.ds(b * 2, 8, stride=32), :]
         x1 = col_wide[pl.ds(b * 2 + 1, 8, stride=32), :]
         r0 = jnp.where(low8, x0, half_swap(x1))
         r1 = jnp.where(low8, half_swap(x0), x1)
         col_next[b] = jnp.concatenate([r0, r1], axis=0).astype(B16)
-        return 0
-
-    lax.fori_loop(0, 16, spread, 0)
     col_plane_c = copies(COL_PLANE, "plane", lambda k: col_next, lambda m: col_plane.at[m])
     col_plane[plane] = col_next[...]
 
     pair_finish(row_pair_c)
     for h in range(2):
-        rows[pl.ds(h * 128, 128), :] = row_pair[:, h].reshape(128, 128)
-    rows_t[...] = rows[...].astype(F32).T.astype(B16)
-    low = lanes((128, 128)) < 64
-
-    def col_grad(b, _):
-        r = dot(rows[...], upstream[b], (1, 0))
-        a = jnp.where(low, r[:128, :128], r[128:, 128:])
-        c = jnp.where(low, r[:128, 128:], r[128:, :128])
-        out = (a + half_swap(c)) * (1.0 / SEQUENCES)
-        colg_send[:, b] = out.astype(B16).reshape(8, 16, 128)
-        return 0
-
-    lax.fori_loop(0, 16, col_grad, 0)
+        rows[:, pl.ds(h * 128, 128)] = row_pair[:, h].reshape(128, 128)
+    for t in range(8):
+        r = (dot(rows[...], upstream[t], (1, 0)) * (1.0 / SEQUENCES)).astype(B16)
+        for h in range(2):
+            colg_send[:, t * 2 + h] = r[:, h * 128 : h * 128 + 128].reshape(8, 16, 128)
     colg_plane_c = copies(COLG_PLANE, "plane", lambda k: colg_send.at[k], lambda m: colg_got.at[m])
     colg_got[plane] = colg_send[plane]
+    rows_t[...] = rows[...].astype(F32).T.astype(B16)
+    pair_two[...] = jnp.zeros((1024, 256), B16)
+    for i in range(8):
+        for h in range(2):
+            pair_two[pl.ds(i * 128 + h * 64, 64), pl.ds(h * 128, 128)] = pair_ref[pl.ds(i * 64, 64), :]
 
     finish(col_plane_c)
-    rowg_acc[...] = jnp.zeros((128, 256), F32)
-
-    def row_grad(b, _):
-        c = col_plane[:, b].reshape(128, 128).astype(F32)
-        s = half_swap(c)
-        cols[b, pl.ds(0, 128), pl.ds(0, 128)] = jnp.where(low, c, 0.0).astype(B16)
-        cols[b, pl.ds(128, 128), pl.ds(0, 128)] = jnp.where(low, 0.0, s).astype(B16)
-        cols[b, pl.ds(0, 128), pl.ds(128, 128)] = jnp.where(low, s, 0.0).astype(B16)
-        cols[b, pl.ds(128, 128), pl.ds(128, 128)] = jnp.where(low, 0.0, c).astype(B16)
-        rowg_acc[...] += dot(upstream[b], cols[b], (1, 1))
-        return 0
-
-    lax.fori_loop(0, 16, row_grad, 0)
-    grad_t = (rowg_acc[...].T * (1.0 / SEQUENCES)).astype(B16)
+
+    def col_tile(t):
+        both = [col_plane[:, t * 2 + h].reshape(128, 128) for h in range(2)]
+        return jnp.concatenate(both, axis=1)
+
+    row_part = dot(col_tile(0), upstream[0], (1, 1))
+    for t in range(1, 8):
+        row_part = row_part + dot(col_tile(t), upstream[t], (1, 1))
+    row_part = (row_part * (1.0 / SEQUENCES)).astype(B16)
     for h in range(2):
-        rowg_send[:, h] = grad_t[h * 128 : h * 128 + 128].reshape(8, 16, 128)
+        rowg_send[:, h] = row_part[:, h * 128 : h * 128 + 128].reshape(8, 16, 128)
 
     def keep_rowg():
         rowg_got[narrow] = rowg_send[plane]
@@ -286,21 +279,16 @@
         ROWG_PAIR, source, narrow, lambda d: rowg_send.at[(plane + d) % 8], rowg_got, keep_rowg
     )
 
-    def outer_prod(b, _):
-        o = (dot(rows_t[...], cols[b], (1, 0)) * (1.0 / SEQUENCES)).astype(B16)
-        for t in range(2):
-            for g in range(4):
-                outer[b * 2 + t, :, pl.ds(g * 128, 128)] = o[g * 32 : g * 32 + 32, t * 128 : t * 128 + 128]
-        return 0
-
-    lax.fori_loop(0, 16, outer_prod, 0)
-
-    def weight_grad(k, _):
-        o = outer[pl.ds(k * 4, 4)].reshape(128, 512)
-        big_send[k] = dot(o, pair_order[...], (1, 0)).astype(B16)
-        return 0
-
-    lax.fori_loop(0, 8, weight_grad, 0)
+    for t in range(8):
+        o = (dot(rows_t[...], col_tile(t), (1, 0)) * (1.0 / SEQUENCES)).astype(B16)
+        for h in range(2):
+            for i in range(8):
+                outer[t * 2 + h, :, pl.ds(i * 128, 128)] = o[i * 32 : i * 32 + 32, h * 128 : h * 128 + 128]
+    for c in range(2):
+        res = dot(outer[pl.ds(c * 8, 8)].reshape(256, 1024), pair_two[...], (1, 0)).astype(B16)
+        for k in range(4):
+            for h in range(2):
+                big_send[c * 4 + k, pl.ds(h * 64, 64), :] = res[k * 64 : k * 64 + 64, h * 128 : h * 128 + 128]
     big_plane_c = copies(BIG_PLANE, "plane", lambda k: big_send.at[k], lambda m: big_plane.at[m])
     big_plane[plane] = big_send[plane]
 
@@ -315,16 +303,13 @@
 
     finish(colg_plane_c)
 
-    def collect(b, _):
+    for b in range(16):
         acc = colg_got[0, b].astype(F32)
         for k in range(1, 8):
             acc = acc + colg_got[k, b].astype(F32)
         y0, y1 = acc[:8], acc[8:]
         colg_wide[pl.ds(b * 2, 8, stride=32), :] = jnp.where(low8, y0, half_swap(y1))
         colg_wide[pl.ds(b * 2 + 1, 8, stride=32), :] = jnp.where(low8, half_swap(y0), y1)
-        return 0
-
-    lax.fori_loop(0, 16, collect, 0)
     colg_next[...] = colg_wide[...].astype(B16).reshape(8, 32, 128)
     colg_depth_c = copies(COLG_DEPTH, "depth", lambda k: colg_next.at[k], lambda m: colg_depth.at[m])
     colg_depth[depth] = colg_next[depth]
@@ -397,7 +382,7 @@
     big_narrow[narrow] = big_two[...]
 
     finish(small_plane_c)
-    small_part[...] = total(small_plane)
+    small_part[...] = total(small_plane).astype(B16)
     small_depth_c = copies(SMALL_DEPTH, "depth", lambda k: small_part, lambda m: small_depth.at[m])
     small_depth[depth] = small_part[...]
 
@@ -407,59 +392,88 @@
     big_back[depth] = big_three[...]
 
     finish(small_depth_c)
-    small_two[...] = total(small_depth)
+    small_two[...] = total(small_depth).astype(B16)
     small_narrow_c = copies(SMALL_NARROW, "narrow", lambda k: small_two, lambda m: small_narrow.at[m])
     small_narrow[narrow] = small_two[...]
 
     finish(big_back_c)
     big_half[...] = big_back[...].astype(B16).reshape(128, 128)
-    big_out_c = copies(BIG_OUT, "plane", lambda k: big_half, lambda m: big_out.at[m])
-    big_out[plane] = big_half[...]
+    big_out_c = copies(BIG_OUT, "plane", lambda k: big_half, lambda m: big_all.at[m])
+    big_all[plane] = big_half[...]
 
     finish(small_narrow_c)
-    small_three[...] = total(small_narrow)
-    small_out_c = copies(SMALL_OUT, "plane", lambda k: small_three, lambda m: strip(small_all, m))
-    small_all[pl.ds(pl.multiple_of(plane * 24, 8), 24), :] = small_three[...]
-
+    small_three[...] = total(small_narrow).astype(B16)
+    small_out_c = copies(SMALL_OUT, "plane", lambda k: small_three, lambda m: small_all.at[m])
+    small_all[plane] = small_three[...]
+
+    finish(big_out_c)
+    for k in range(8):
+        for h in range(2):
+            for b in range(2):
+                piece = big_all[k, pl.ds((h * 2 + b) * 32, 32), :].astype(F32)
+                weight_out[pl.ds(k * 4 + b * 2 + h, 32, stride=32), :] = piece
     finish(small_out_c)
-    proj_out[:, pl.ds(0, 128)] = small_all[pl.ds(0, 64), :]
-    proj_out[:, pl.ds(128, 128)] = small_all[pl.ds(64, 64), :]
-    norm_out[:, pl.ds(0, 128)] = small_all[pl.ds(128, 2, stride=2), :]
-    norm_out[:, pl.ds(128, 128)] = small_all[pl.ds(129, 2, stride=2), :]
-    bias_out[...] = small_all[pl.ds(132, 2), pl.ds(0, 32)]
-    finish(big_out_c)
+    small = small_all[...].astype(F32).reshape(192, 128)
+    proj_out[:, pl.ds(0, 128)] = small[0:64]
+    proj_out[:, pl.ds(128, 128)] = small[64:128]
+    norm_out[0:1, pl.ds(0, 128)] = small[128:129]
+    norm_out[0:1, pl.ds(128, 128)] = small[129:130]
+    norm_out[1:2, pl.ds(0, 128)] = small[130:131]
+    norm_out[1:2, pl.ds(128, 128)] = small[131:132]
+    bias_out[...] = small[132:134, :32]
+
+
+def put_kernel(*refs):
+    sem = refs[10]
+    made = [pltpu.make_async_copy(refs[k], refs[5 + k], sem.at[k]) for k in range(5)]
+    for c in made:
+        c.start()
+    for c in made:
+        c.wait()
+
+
+def put(results):
+    return pl.pallas_call(
+        put_kernel,
+        out_shape=tuple(jax.ShapeDtypeStruct(r.shape, r.dtype) for r in results),
+        in_specs=[pl.BlockSpec(memory_space=pltpu.VMEM)] * 5,
+        out_specs=(pl.BlockSpec(memory_space=pl.ANY),) * 5,
+        scratch_shapes=[pltpu.SemaphoreType.DMA((5,))],
+    )(*[pltpu.with_memory_space_constraint(r, pltpu.VMEM) for r in results])
 
 
 def everything(x, pair, gain, shift, weight, bias, out_weight):
     vmem = pl.BlockSpec(memory_space=pltpu.VMEM)
+    hbm = pl.BlockSpec(memory_space=pl.ANY)
     scratch = [
         ((128, 256), F32), ((128, 256), B16), ((2, 128, 128), F32), ((128, 128), F32), ((32, 128), F32),
         ((64, 128), F32), ((32, 128), B16), ((64, 128), F32), ((8, 32, 128), B16), ((256, 128), F32),
         ((2, 16, 128), B16), ((16, 16, 128), B16),
-        ((8, 2, 16, 128), B16), ((8, 16, 16, 128), B16), ((512, 128), B16), ((1024, 128), F32),
-        ((32, 32, 128), B16), ((16, 128, 256), B16), ((256, 128), B16), ((128, 256), B16),
-        ((16, 256, 256), B16), ((32, 32, 512), B16),
-        ((8, 16, 16, 128), B16), ((8, 16, 16, 128), B16), ((128, 256), F32), ((8, 2, 16, 128), B16),
+        ((8, 2, 16, 128), B16), ((8, 16, 16, 128), B16), ((512, 128), B16), ((1024, 128), B16), ((1024, 256), B16),
+        ((1024, 128), F32), ((1024, 128), B16), ((8, 256, 256), B16), ((128, 256), B16), ((256, 128), B16),
+        ((16, 32, 1024), B16),
+        ((8, 16, 16, 128), B16), ((8, 16, 16, 128), B16), ((8, 2, 16, 128), B16),
         ((8, 2, 16, 128), B16), ((64, 128), F32), ((64, 128), F32), ((32, 128), F32),
         ((256, 128), F32), ((8, 32, 128), B16), ((8, 32, 128), B16), ((2, 128, 128), F32),
         ((8, 128, 128), B16), ((8, 128, 128), B16), ((8, 16, 128), F32), ((8, 16, 128), F32), ((16, 128), F32),
         ((8, 16, 128), F32), ((16, 128), F32), ((8, 16, 128), F32), ((128, 128), B16),
-        ((192, 128), F32), ((8, 24, 128), F32), ((24, 128), F32), ((8, 24, 128), F32), ((24, 128), F32),
-        ((8, 24, 128), F32), ((24, 128), F32), ((192, 128), F32),
+        ((8, 128, 128), B16),
+        ((192, 128), F32), ((8, 24, 128), F32), ((24, 128), B16), ((8, 24, 128), B16), ((24, 128), B16),
+        ((8, 24, 128), B16), ((24, 128), B16), ((8, 24, 128), B16),
     ]
     return pl.pallas_call(
         kernel,
         out_shape=(
-            jax.ShapeDtypeStruct((128, 256), B16),
-            jax.ShapeDtypeStruct((64, 256), F32),
-            jax.ShapeDtypeStruct((2, 32), F32),
-            jax.ShapeDtypeStruct((2, 256), F32),
-            jax.ShapeDtypeStruct((8, 128, 128), B16),
+            pltpu.VMEM((128, 256), B16),
+            pltpu.VMEM((64, 256), F32),
+            pltpu.VMEM((2, 32), F32),
+            pltpu.VMEM((2, 256), F32),
+            pltpu.VMEM((1024, 128), F32),
         ),
-        in_specs=[vmem] * 7,
+        in_specs=[vmem, hbm, vmem, vmem, vmem, vmem, hbm],
         out_specs=(vmem,) * 5,
         scratch_shapes=[pltpu.VMEM(shape, kind) for shape, kind in scratch]
-        + [pltpu.SemaphoreType.DMA((STAGES, 8)), pltpu.SemaphoreType.DMA((STAGES, 8))],
+        + [pltpu.SemaphoreType.DMA((STAGES, 8)), pltpu.SemaphoreType.DMA((STAGES, 8)), pltpu.SemaphoreType.DMA((2,))],
         compiler_params=pltpu.CompilerParams(
             collective_id=0, has_side_effects=True, vmem_limit_bytes=56 * 1024 * 1024
         ),
@@ -475,7 +489,7 @@
     projection_bias,
     output_weight,
 ):
-    align, proj, bias, norm, big = everything(
+    results = everything(
         alignment_rows.reshape(128, 256),
         pair_output_gradient.reshape(512, 128),
         layer_norm_gain.reshape(1, 256),
@@ -484,12 +498,12 @@
         projection_bias,
         output_weight,
     )
-    weight_grad = jnp.transpose(big.reshape(32, 32, 128), (1, 0, 2)).reshape(1024, 128)
+    align, proj, bias, norm, weight_grad = put(results)
     return (
         align.reshape(2, 64, 256),
         jnp.transpose(proj.reshape(2, 32, 256), (0, 2, 1)),
         bias,
-        weight_grad.astype(F32),
+        weight_grad,
         norm,
     )
 

time: 77.4 us -> 67.8 us (0.88)
  Pallas kernels: 71.6 us -> 67 us
  local copies, waits for them, and re-layouts: 3.88 us -> 0 us
  other arithmetic: 1 us -> 0 us
    pallas_call x1 -> x2, Pallas kernels: 71.6 us -> 67 us  [the longest x1 66.1 us: everything(): pl.pallas_call(kernel, out_shape=(pltpu.VMEM((128, 256), B16), pltpu.VMEM...]
    unnamed x12 -> x0, local copies, waits for them, and re-layouts: 2.78 us -> none
    convert_element_type x1 -> x0, local copies, waits for them, and re-layouts: 1.1 us -> none  [shards(): weight_grad.astype(F32)]
    convert_element_type x1 -> x0, other arithmetic: 1 us -> none  [shards(): weight_grad.astype(F32)]
where the time goes in v3:
time: 67.8 us; the launch traced here: 67.7 us
  Pallas kernels  67 us (99%)
    pallas_call x1, Pallas kernels, everything(): pl.pallas_call(kernel, out_shape=(pltpu.VMEM((128, 256), B16), pltpu.VMEM...  66.1 us

profile of v3, /device:TPU:1, one launch (start us, length us, event | category | flops | bytes accessed | tf_op | source)
XLA Modules:
  0.0 67.7 jit_solution(12508940109102181660)
XLA Ops:
  0.6 66.1 %shard_map.110 = (bf16[128,256]{1,0:T(8,128)(2,1)S(1)}, f32[64,256]{1,0:T(8,128)S(1)}, f32[2,32]{1,0:T(2,128)S(1)}, f32[2,256]{1,0:T(2,128)S(1)}, f32[1024,128]{1,0:T(8,128)S(1)}) custom-call(bf16[128,256]{1,0:T(8,128)(2,1)} %bitcast.12, bf16[512,128]{1,0:T(8,128)(2,1)} %bitcast.11, f32[1,256]{1,0:T(1,128)} %bitcast.14, f32[1,256]{1,0:T(1,128)} %bitcast.15, ...), custom_call_target="tpu_custom_call" | custom-call | tf_op jit(solution)/shard_map/pallas_call | solution.py:464
  66.8 0.9 %shard_map.111 = (bf16[128,256]{1,0:T(8,128)(2,1)}, f32[64,256]{1,0:T(8,128)}, f32[2,32]{1,0:T(2,128)}, f32[2,256]{1,0:T(2,128)}, f32[1024,128]{1,0:T(8,128)}) custom-call(bf16[128,256]{1,0:T(8,128)(2,1)S(1)} %get-tuple-element.15.refs_0_, f32[64,256]{1,0:T(8,128)S(1)} %get-tuple-element.16.refs_1_, f32[2,32]{1,0:T(2,128)S(1)} %get-tuple-element.17.refs_2_, ...), custom_call_target="tpu_custom_call" | custom-call | tf_op jit(solution)/shard_map/pallas_call | solution.py:436

commit v4 on v3

v4 whole, which is shorter than its diff:
```python
import jax
import jax.numpy as jnp
from jax import lax
from jax.experimental import pallas as pl
from jax.experimental.pallas import tpu as pltpu
from jax.sharding import PartitionSpec as P

F32, B16 = jnp.float32, jnp.bfloat16
MESH_ID = pl.DeviceIdType.MESH
OFFSETS = (4, 3, 5, 2, 6, 1, 7)
STAGES = 20
SEQUENCES = 128
(
    ROW_DEPTH, COL_DEPTH, ROW_PAIR, COL_PLANE, COLG_PLANE, ROWG_PAIR, BIG_PLANE, ROWG_DEPTH, COLG_DEPTH,
    BIG_DEPTH, SMALL_PLANE, BIG_NARROW, SMALL_DEPTH, BIG_BACK, SMALL_NARROW, BIG_OUT, SMALL_OUT,
    PAIR_HALF, ROW_CORE, ROWG_CORE,
) = range(STAGES)


def dot(a, b, dims):
    return lax.dot_general(a, b, ((dims[:1], dims[1:]), ((), ())), preferred_element_type=F32)


def total(ref):
    acc = ref[0].astype(F32)
    for k in range(1, 8):
        acc = acc + ref[k].astype(F32)
    return acc


def lanes(shape):
    return lax.broadcasted_iota(jnp.int32, shape, len(shape) - 1)


def half_swap(x):
    return pltpu.roll(x, 64, 1)


def kernel(
    x_ref, pair_hbm, gain_ref, shift_ref, weight_ref, bias_ref, out_weight_hbm,
    align_out, proj_out, bias_out, norm_out, weight_out,
    normed, scaled, scaled32, inverse, row_tmp,
    row_send, col_send, row_got, col_got, col_wide, row_next, col_next,
    row_pair, col_plane, pair_ref, pair_tile, out_weight_ref, pair_two, weight32, weight_order, upstream, rows, rows_t, outer,
    colg_send, colg_got, rowg_acc, rowg_core, rowg_sum, rowg_send, rowg_got, rowg_next, rowg_depth, rowg,
    colg_wide, colg_next, colg_depth, scaled_grad,
    big_send, big_plane, big_part, big_depth, big_two, big_narrow, big_three, big_back, big_half, big_all,
    small_in, small_plane, small_part, small_depth, small_two, small_narrow, small_three, small_all,
    send_sem, recv_sem, local_sem,
):
    wide = lax.axis_index("wide")
    narrow = lax.axis_index("narrow")
    plane = wide // 8
    depth = wide % 8
    own_pair = plane == narrow
    other_pair = plane != narrow
    lead = plane % 2 == narrow % 2
    follow = plane % 2 != narrow % 2
    barrier = pltpu.get_barrier_semaphore()
    fetch_pair = pltpu.make_async_copy(pair_hbm, pair_ref, local_sem.at[0])
    fetch_weight = pltpu.make_async_copy(out_weight_hbm, out_weight_ref, local_sem.at[1])
    fetch_pair.start()
    fetch_weight.start()
    place = {"plane": plane, "depth": depth, "narrow": narrow}

    def peer(kind, k):
        if kind == "plane":
            return (k * 8 + depth, narrow)
        if kind == "depth":
            return (plane * 8 + k, narrow)
        return (wide, k)

    def holder(d):
        return (narrow * 8 + depth, (narrow + 2 * d) % 8)

    def source(d):
        return (((plane + d) % 8) * 8 + depth, plane)

    def greet(device):
        pl.semaphore_signal(barrier, 1, device_id=device, device_id_type=MESH_ID)

    for kind in ("plane", "depth", "narrow"):
        for d in OFFSETS:
            greet(peer(kind, (place[kind] + d) % 8))
    for d in range(1, 4):
        greet(holder(d))

    @pl.when(lead)
    def _():
        for d in range(1, 8):
            greet(source(d))

    @pl.when(lead & other_pair)
    def _():
        greet(source(0))

    @pl.when(other_pair)
    def _():
        greet(holder(0))

    def copies(stage, kind, give, target, size=1):
        me = place[kind]
        lead = pl.ds(pl.multiple_of(me * size, size), size) if size > 1 else me
        for d in OFFSETS:
            k = (me + d) % 8
            pltpu.make_async_remote_copy(
                src_ref=give(k),
                dst_ref=target.at[lead],
                send_sem=send_sem.at[stage],
                recv_sem=recv_sem.at[stage],
                device_id=peer(kind, k),
                device_id_type=MESH_ID,
            ).start()
        whole = target.at[pl.ds(0, 7 * size)]
        return pltpu.make_async_remote_copy(
            src_ref=whole,
            dst_ref=whole,
            send_sem=send_sem.at[stage],
            recv_sem=recv_sem.at[stage],
            device_id=peer(kind, (me + 1) % 8),
            device_id_type=MESH_ID,
        )

    def finish(c):
        c.wait()

    def sent(stage, device, source_ref, target_ref):
        return pltpu.make_async_remote_copy(
            src_ref=source_ref,
            dst_ref=target_ref,
            send_sem=send_sem.at[stage],
            recv_sem=recv_sem.at[stage],
            device_id=device,
            device_id_type=MESH_ID,
        )

    partner = (wide, narrow + 1 - 2 * (narrow % 2))

    def for_own(what):
        pl.when(own_pair)(lambda: what(True))
        pl.when(other_pair)(lambda: what(False))

    value = x_ref[...].astype(F32)
    centre = value - jnp.mean(value, axis=-1, keepdims=True)
    inv = lax.rsqrt(jnp.mean(centre * centre, axis=-1, keepdims=True) + 1e-05)
    norm = centre * inv
    inverse[...] = jnp.broadcast_to(inv, (128, 128))
    normed[...] = norm
    scaled_b = (norm * gain_ref[...] + shift_ref[...]).astype(B16)
    scaled[...] = scaled_b
    for c in range(2):
        scaled32[c] = scaled_b[:, c * 128 : c * 128 + 128].astype(F32)

    def every_fourth(g):
        both = [scaled32[c, pl.ds(g, 32, stride=4), :] for c in range(2)]
        return jnp.concatenate(both, axis=1).astype(B16)

    w_row = weight_ref[0:32, :]
    w_col = weight_ref[32:64, :]
    w_row4 = jnp.concatenate([w_row] * 4, axis=0)
    sub = lax.broadcasted_iota(jnp.int32, (32, 32), 0)
    diagonal = sub == lanes((32, 32))
    row_bias = jnp.sum(jnp.where(diagonal, bias_ref[0:1, :], 0.0), axis=1, keepdims=True)
    col_bias = jnp.sum(jnp.where(diagonal, bias_ref[1:2, :], 0.0), axis=1, keepdims=True)
    lane128 = lanes((32, 128))
    sub128 = lax.broadcasted_iota(jnp.int32, (32, 128), 0)
    row_bias4 = jnp.sum(jnp.where(sub128 == lane128 % 32, row_bias, 0.0), axis=0, keepdims=True)
    group = lane128 // 32
    row_fac = jnp.zeros((32, 128), F32)
    for g in range(4):
        row_fac = jnp.where(group == g, dot(every_fourth(g), w_row4, (1, 1)), row_fac)
    row_tmp[...] = (row_fac + row_bias4).astype(B16).astype(F32)
    for g in range(4):
        for r in range(2):
            row_send[pl.ds(g * 8 + r * 4, 4), :] = row_tmp[pl.ds(r * 16 + g * 4, 4), :]
    even_lane = lanes((16, 128)) // 32 % 2 == 0
    col_fac = dot(w_col, scaled_b, (1, 1)) + col_bias
    fac_a, fac_b = col_fac[:16], col_fac[16:]
    col_send[0] = jnp.where(even_lane, fac_a, pltpu.roll(fac_b, 32, 1)).astype(B16)
    col_send[1] = jnp.where(even_lane, pltpu.roll(fac_a, 96, 1), fac_b).astype(B16)
    pl.semaphore_wait(barrier, 25 + jnp.where(lead, 8, 0) - jnp.where(own_pair, 2, 0))

    def eight(ref, k):
        return ref.at[pl.ds(pl.multiple_of(k * 8, 8), 8)]

    parity = depth % 2
    row_depth_c = copies(ROW_DEPTH, "depth", lambda k: eight(row_send, k // 2), row_got, 8)
    col_depth_c = copies(COL_DEPTH, "depth", lambda k: col_send.at[k % 2], col_got)
    mine = pl.ds(pl.multiple_of(depth * 8, 8), 8)
    row_got[mine, :] = row_send[pl.ds(pl.multiple_of(depth // 2 * 8, 8), 8), :]
    col_got[depth] = col_send[parity]
    fetch_pair.wait()
    own_rows = pl.ds(pl.multiple_of(parity * 8, 8), 8)
    pair_half_c = pltpu.make_async_remote_copy(
        src_ref=pair_ref.at[:, pl.ds(pl.multiple_of((1 - parity) * 32, 32), 32)],
        dst_ref=pair_tile.at[own_rows],
        send_sem=send_sem.at[PAIR_HALF],
        recv_sem=recv_sem.at[PAIR_HALF],
        device_id=peer("depth", depth + 1 - 2 * parity),
        device_id_type=MESH_ID,
    )
    pair_half_c.start()
    pair_tile[own_rows] = pair_ref[:, pl.ds(pl.multiple_of(parity * 32, 32), 32), :]

    fetch_weight.wait()
    weight32[...] = out_weight_ref[...].astype(F32)
    for b in range(8):
        for c in range(4):
            q = c % 2 * 16 + b * 2 + c // 2
            weight_order[pl.ds((b * 4 + c) * 32, 32), :] = weight32[pl.ds(q, 32, stride=32), :].astype(B16)

    finish(row_depth_c)
    for g in range(4):
        both = [row_got[pl.ds(r * 4 + g, 8, stride=8), :] for r in range(2)]
        row_next[g] = jnp.concatenate(both, axis=0).astype(B16)

    for d in range(1, 4):
        sent(ROW_PAIR, holder(d), row_next, row_pair.at[plane]).start()

    @pl.when(other_pair)
    def _():
        sent(ROW_PAIR, holder(0), row_next, row_pair.at[plane]).start()

    @pl.when(own_pair)
    def _():
        row_pair[plane] = row_next[...]

    finish(col_depth_c)
    col_wide[...] = col_got[...].astype(F32).reshape(128, 128)
    low8 = lanes((8, 128)) < 64

    for b in range(8):
        x0 = col_wide[pl.ds(b * 2, 8, stride=16), :]
        x1 = col_wide[pl.ds(b * 2 + 1, 8, stride=16), :]
        r0 = jnp.where(low8, x0, half_swap(x1))
        r1 = jnp.where(low8, half_swap(x0), x1)
        col_next[b] = jnp.concatenate([r0, r1], axis=0).astype(B16)
    col_plane_c = copies(COL_PLANE, "plane", lambda k: col_next, col_plane)
    col_plane[plane] = col_next[...]

    low32 = lane128 < 64
    even32 = group % 2 == 0
    pair_half_c.wait()

    def up(t, _):
        tile = pair_tile[...].reshape(512, 128)
        for h in range(2):
            w = weight_order[pl.ds(pl.multiple_of(t * 256 + h * 128, 128), 128), :]
            res = dot(w, tile, (1, 1))
            for i in range(4):
                a = [res[c * 32 : c * 32 + 32, i * 128 : i * 128 + 128] for c in range(4)]
                first = [jnp.where(low32, a[c], half_swap(a[c + 2])) for c in range(2)]
                second = [jnp.where(low32, half_swap(a[c]), a[c + 2]) for c in range(2)]
                out = []
                for f in (first, second):
                    out.append(jnp.where(even32, f[0], pltpu.roll(f[1], 32, 1)))
                    out.append(jnp.where(even32, pltpu.roll(f[0], 96, 1), f[1]))
                upstream[t, pl.ds(i * 128, 128), pl.ds(h * 128, 128)] = jnp.concatenate(out, axis=0).astype(B16)
        return 0

    lax.fori_loop(0, 4, up, 0)

    pair_two[...] = jnp.zeros((2048, 512), B16)
    for i in range(16):
        for c in range(4):
            pair_two[pl.ds(i * 128 + c * 32, 32), pl.ds(c * 128, 128)] = pair_tile[i]

    def sent_rows(own):
        part = row_pair.at[pl.ds(0, 3 if own else 4)]
        sent(ROW_PAIR, partner, part, part).wait_send()

    for_own(sent_rows)

    @pl.when(lead)
    def _():
        def came(own):
            part = row_pair.at[pl.ds(0, 7 if own else 8)]
            sent(ROW_PAIR, partner, part, part).wait_recv()

        for_own(came)
        sent(ROW_CORE, partner, row_pair, row_pair).start()

    @pl.when(follow)
    def _():
        sent(ROW_CORE, partner, row_pair, row_pair).wait_recv()

    for g in range(4):
        rows[:, pl.ds(g * 128, 128)] = row_pair[:, g].reshape(128, 128)
    for t in range(4):
        r = (dot(rows[...], upstream[t], (1, 0)) * (1.0 / SEQUENCES)).astype(B16)
        for h in range(2):
            colg_send[:, t * 2 + h] = r[:, h * 128 : h * 128 + 128].reshape(8, 16, 128)
    colg_plane_c = copies(COLG_PLANE, "plane", lambda k: colg_send.at[k], colg_got)
    colg_got[plane] = colg_send[plane]
    rows_t[...] = rows[...].astype(F32).T.astype(B16)
    finish(col_plane_c)

    def col_tile(t):
        both = [col_plane[:, t * 2 + h].reshape(128, 128) for h in range(2)]
        return jnp.concatenate(both, axis=1)

    row_part = dot(col_tile(0), upstream[0], (1, 1))
    for t in range(1, 4):
        row_part = row_part + dot(col_tile(t), upstream[t], (1, 1))
    row_part = row_part * (1.0 / SEQUENCES)
    rowg_acc[...] = row_part
    row_part = row_part.astype(B16)
    for g in range(4):
        rowg_send[:, g] = row_part[:, g * 128 : g * 128 + 128].reshape(8, 16, 128)

    @pl.when(follow)
    def _():
        sent(ROWG_CORE, partner, rowg_send, rowg_core).start()

    for t in range(4):
        o = (dot(rows_t[...], col_tile(t), (1, 0)) * (1.0 / SEQUENCES)).astype(B16)
        for h in range(2):
            for i in range(16):
                outer[t * 2 + h, :, pl.ds(i * 128, 128)] = o[i * 32 : i * 32 + 32, h * 128 : h * 128 + 128]

    @pl.when(lead)
    def _():
        sent(ROWG_CORE, partner, rowg_send, rowg_core).wait_recv()
        for g in range(4):
            both = rowg_acc[:, pl.ds(g * 128, 128)] + rowg_core[:, g].reshape(128, 128).astype(F32)
            rowg_sum[:, g] = both.astype(B16).reshape(8, 16, 128)
        for d in range(1, 8):
            sent(ROWG_PAIR, source(d), rowg_sum.at[(plane + d) % 8], rowg_got.at[narrow // 2]).start()

    @pl.when(lead & other_pair)
    def _():
        sent(ROWG_PAIR, source(0), rowg_sum.at[plane], rowg_got.at[narrow // 2]).start()

    @pl.when(own_pair)
    def _():
        rowg_got[narrow // 2] = rowg_sum[plane]

    for g in range(2):
        res = dot(outer[pl.ds(g * 4, 4)].reshape(128, 2048), pair_two[...], (1, 0)).astype(B16)
        for k in range(4):
            for c in range(4):
                big_send[g * 4 + k, pl.ds(c * 32, 32), :] = res[k * 32 : k * 32 + 32, c * 128 : c * 128 + 128]
    big_plane_c = copies(BIG_PLANE, "plane", lambda k: big_send.at[k], big_plane)
    big_plane[plane] = big_send[plane]

    def came_rowg(own):
        part = rowg_got.at[pl.ds(0, 3 if own else 4)]
        sent(ROWG_PAIR, partner, part, part).wait_recv()

    for_own(came_rowg)
    row_sum = rowg_got[0].astype(F32)
    for k in range(1, 4):
        row_sum = row_sum + rowg_got[k].astype(F32)
    for g in range(4):
        for r in range(2):
            rowg_next[pl.ds(r * 4 + g, 8, stride=8), :] = row_sum[g, r * 8 : r * 8 + 8, :]
    rowg_depth_c = copies(ROWG_DEPTH, "depth", lambda k: eight(rowg_next, k), rowg_depth, 8)
    rowg_depth[mine, :] = rowg_next[mine, :]

    finish(colg_plane_c)

    for b in range(8):
        acc = colg_got[0, b].astype(F32)
        for k in range(1, 8):
            acc = acc + colg_got[k, b].astype(F32)
        y0, y1 = acc[:8], acc[8:]
        colg_wide[pl.ds(b * 2, 8, stride=16), :] = jnp.where(low8, y0, half_swap(y1))
        colg_wide[pl.ds(b * 2 + 1, 8, stride=16), :] = jnp.where(low8, half_swap(y0), y1)
    colg_next[...] = colg_wide[...].astype(B16).reshape(8, 16, 128)
    colg_depth_c = copies(COLG_DEPTH, "depth", lambda k: colg_next.at[k], colg_depth)
    colg_depth[depth] = colg_next[depth]

    finish(big_plane_c)
    big_part[...] = total(big_plane).astype(B16).reshape(8, 16, 128)
    big_depth_c = copies(BIG_DEPTH, "depth", lambda k: big_part.at[k], big_depth)
    big_depth[depth] = big_part[depth]

    finish(rowg_depth_c)
    for g in range(4):
        for r in range(2):
            one = rowg_depth[pl.ds(g * 16 + r * 4, 4), :] + rowg_depth[pl.ds(g * 16 + 8 + r * 4, 4), :]
            rowg[pl.ds(r * 16 + g * 4, 4), :] = one
    row_g = rowg[...]
    row_gb = row_g.astype(B16)
    row_fold = jnp.sum(row_g, axis=0, keepdims=True)
    row_fold = row_fold + pltpu.roll(row_fold, 32, 1) + pltpu.roll(row_fold, 64, 1) + pltpu.roll(row_fold, 96, 1)
    finish(colg_depth_c)
    half = []
    for h in range(2):
        one = colg_depth[h].astype(F32)
        for k in range(1, 4):
            one = one + colg_depth[k * 2 + h].astype(F32)
        half.append(one)
    col_g = jnp.concatenate(
        [
            jnp.where(even_lane, half[0], pltpu.roll(half[1], 32, 1)),
            jnp.where(even_lane, pltpu.roll(half[0], 96, 1), half[1]),
        ],
        axis=0,
    )
    col_gb = col_g.astype(B16)
    col_sum = jnp.sum(col_g, axis=1, keepdims=True)
    col_fold = jnp.sum(jnp.where(sub128 == lane128, col_sum, 0.0), axis=0, keepdims=True)
    from_cols = dot(col_gb, w_col, (0, 0))
    for c in range(2):
        scaled_grad[c] = from_cols[:, c * 128 : c * 128 + 128]
    proj_col = dot(col_gb, scaled[...], (1, 0))
    proj_row4 = jnp.zeros((128, 256), F32)
    for g in range(4):
        masked = jnp.where(group == g, row_gb.astype(F32), 0.0).astype(B16)
        more = dot(masked, w_row4, (1, 0))
        for c in range(2):
            spot = (c, pl.ds(g, 32, stride=4), slice(None))
            scaled_grad[spot] = scaled_grad[spot] + more[:, c * 128 : c * 128 + 128]
        proj_row4 = proj_row4 + dot(masked, every_fourth(g), (0, 0))
    proj_row = proj_row4[0:32] + proj_row4[32:64] + proj_row4[64:96] + proj_row4[96:128]
    grad = jnp.concatenate([scaled_grad[0], scaled_grad[1]], axis=1)
    norm = normed[...]
    gain_grad = jnp.sum(grad * norm, axis=0, keepdims=True)
    shift_grad = jnp.sum(grad, axis=0, keepdims=True)
    small_in[pl.ds(0, 32), :] = proj_row[:, :128]
    small_in[pl.ds(32, 32), :] = proj_col[:, :128]
    small_in[pl.ds(64, 32), :] = proj_row[:, 128:]
    small_in[pl.ds(96, 32), :] = proj_col[:, 128:]
    small_in[pl.ds(128, 64), :] = jnp.zeros((64, 128), F32)
    small_in[pl.ds(128, 1), :] = gain_grad[:, :128]
    small_in[pl.ds(129, 1), :] = gain_grad[:, 128:]
    small_in[pl.ds(130, 1), :] = shift_grad[:, :128]
    small_in[pl.ds(131, 1), :] = shift_grad[:, 128:]
    small_in[pl.ds(132, 1), :] = row_fold
    small_in[pl.ds(133, 1), :] = col_fold

    def strip(ref, k):
        return ref.at[pl.ds(pl.multiple_of(k * 24, 8), 24)]

    small_plane_c = copies(SMALL_PLANE, "plane", lambda k: strip(small_in, k), small_plane)
    small_plane[plane] = small_in[pl.ds(pl.multiple_of(plane * 24, 8), 24), :]

    inv = inverse[...][:, :1]
    gained = grad * gain_ref[...]
    align = inv * (
        gained
        - jnp.mean(gained, axis=-1, keepdims=True)
        - norm * jnp.mean(gained * norm, axis=-1, keepdims=True)
    )
    align_out[...] = align.astype(B16)

    finish(big_depth_c)
    big_two[...] = total(big_depth).astype(B16)
    big_narrow_c = copies(BIG_NARROW, "narrow", lambda k: big_two, big_narrow)
    big_narrow[narrow] = big_two[...]

    finish(small_plane_c)
    small_part[...] = total(small_plane).astype(B16)
    small_depth_c = copies(SMALL_DEPTH, "depth", lambda k: small_part, small_depth)
    small_depth[depth] = small_part[...]

    finish(big_narrow_c)
    big_three[...] = total(big_narrow).astype(B16)
    big_back_c = copies(BIG_BACK, "depth", lambda k: big_three, big_back)
    big_back[depth] = big_three[...]

    finish(small_depth_c)
    small_two[...] = total(small_depth).astype(B16)
    small_narrow_c = copies(SMALL_NARROW, "narrow", lambda k: small_two, small_narrow)
    small_narrow[narrow] = small_two[...]

    finish(big_back_c)
    big_half[...] = big_back[...].reshape(128, 128)
    big_out_c = copies(BIG_OUT, "plane", lambda k: big_half, big_all)
    big_all[plane] = big_half[...]

    finish(small_narrow_c)
    small_three[...] = total(small_narrow).astype(B16)
    small_out_c = copies(SMALL_OUT, "plane", lambda k: small_three, small_all)
    small_all[plane] = small_three[...]

    finish(big_out_c)
    for k in range(8):
        for c in range(4):
            piece = big_all[k, pl.ds(c * 32, 32), :].astype(F32)
            weight_out[pl.ds(c % 2 * 16 + k * 2 + c // 2, 32, stride=32), :] = piece
    @pl.when(lead)
    def _():
        sent(ROW_CORE, partner, row_pair, row_pair).wait_send()

        def sent_sums(own):
            part = rowg_sum.at[pl.ds(0, 7 if own else 8)]
            sent(ROWG_PAIR, partner, part, part).wait_send()

        for_own(sent_sums)

    @pl.when(follow)
    def _():
        sent(ROWG_CORE, partner, rowg_send, rowg_core).wait_send()

    finish(small_out_c)
    small = small_all[...].astype(F32).reshape(192, 128)
    proj_out[:, pl.ds(0, 128)] = small[0:64]
    proj_out[:, pl.ds(128, 128)] = small[64:128]
    norm_out[0:1, pl.ds(0, 128)] = small[128:129]
    norm_out[0:1, pl.ds(128, 128)] = small[129:130]
    norm_out[1:2, pl.ds(0, 128)] = small[130:131]
    norm_out[1:2, pl.ds(128, 128)] = small[131:132]
    bias_out[...] = small[132:134, :32]


def put_kernel(*refs):
    sem = refs[10]
    made = [pltpu.make_async_copy(refs[k], refs[5 + k], sem.at[k]) for k in range(5)]
    for c in made:
        c.start()
    for c in made:
        c.wait()


def put(results):
    return pl.pallas_call(
        put_kernel,
        out_shape=tuple(jax.ShapeDtypeStruct(r.shape, r.dtype) for r in results),
        in_specs=[pl.BlockSpec(memory_space=pltpu.VMEM)] * 5,
        out_specs=(pl.BlockSpec(memory_space=pl.ANY),) * 5,
        scratch_shapes=[pltpu.SemaphoreType.DMA((5,))],
    )(*[pltpu.with_memory_space_constraint(r, pltpu.VMEM) for r in results])


def everything(x, pair, gain, shift, weight, bias, out_weight):
    vmem = pl.BlockSpec(memory_space=pltpu.VMEM)
    hbm = pl.BlockSpec(memory_space=pl.ANY)
    scratch = [
        ((128, 256), F32), ((128, 256), B16), ((2, 128, 128), F32), ((128, 128), F32), ((32, 128), F32),
        ((32, 128), F32), ((2, 16, 128), B16), ((64, 128), F32), ((8, 16, 128), B16), ((128, 128), F32),
        ((4, 16, 128), B16), ((8, 16, 128), B16),
        ((8, 4, 16, 128), B16), ((8, 8, 16, 128), B16), ((8, 64, 128), B16), ((16, 32, 128), B16), ((1024, 128), B16),
        ((2048, 512), B16), ((1024, 128), F32), ((1024, 128), B16), ((4, 512, 256), B16), ((128, 512), B16),
        ((512, 128), B16), ((8, 32, 2048), B16),
        ((8, 8, 16, 128), B16), ((8, 8, 16, 128), B16), ((128, 512), F32), ((8, 4, 16, 128), B16), ((8, 4, 16, 128), B16),
        ((8, 4, 16, 128), B16),
        ((4, 4, 16, 128), B16), ((64, 128), F32), ((64, 128), F32), ((32, 128), F32),
        ((128, 128), F32), ((8, 16, 128), B16), ((8, 16, 128), B16), ((2, 128, 128), F32),
        ((8, 128, 128), B16), ((8, 128, 128), B16), ((8, 16, 128), B16), ((8, 16, 128), B16), ((16, 128), B16),
        ((8, 16, 128), B16), ((16, 128), B16), ((8, 16, 128), B16), ((128, 128), B16),
        ((8, 128, 128), B16),
        ((192, 128), F32), ((8, 24, 128), F32), ((24, 128), B16), ((8, 24, 128), B16), ((24, 128), B16),
        ((8, 24, 128), B16), ((24, 128), B16), ((8, 24, 128), B16),
    ]
    return pl.pallas_call(
        kernel,
        out_shape=(
            pltpu.VMEM((128, 256), B16),
            pltpu.VMEM((64, 256), F32),
            pltpu.VMEM((2, 32), F32),
            pltpu.VMEM((2, 256), F32),
            pltpu.VMEM((1024, 128), F32),
        ),
        in_specs=[vmem, hbm, vmem, vmem, vmem, vmem, hbm],
        out_specs=(vmem,) * 5,
        scratch_shapes=[pltpu.VMEM(shape, kind) for shape, kind in scratch]
        + [pltpu.SemaphoreType.DMA((STAGES,)), pltpu.SemaphoreType.DMA((STAGES,)), pltpu.SemaphoreType.DMA((2,))],
        compiler_params=pltpu.CompilerParams(
            collective_id=0, has_side_effects=True, vmem_limit_bytes=56 * 1024 * 1024
        ),
    )(x, pair, gain, shift, weight, bias, out_weight)


def shards(
    alignment_rows,
    pair_output_gradient,
    layer_norm_gain,
    layer_norm_bias,
    projection_weight,
    projection_bias,
    output_weight,
):
    results = everything(
        alignment_rows.reshape(128, 256),
        pair_output_gradient,
        layer_norm_gain.reshape(1, 256),
        layer_norm_bias.reshape(1, 256),
        jnp.transpose(projection_weight, (0, 2, 1)).reshape(64, 256),
        projection_bias,
        output_weight,
    )
    align, proj, bias, norm, weight_grad = put(results)
    return (
        align.reshape(2, 64, 256),
        jnp.transpose(proj.reshape(2, 32, 256), (0, 2, 1)),
        bias,
        weight_grad,
        norm,
    )


def solution(mesh):
    return jax.shard_map(
        shards,
        mesh=mesh,
        in_specs=(P("wide", "narrow", None), P("wide", "narrow", None), P(), P(), P(), P(), P()),
        out_specs=(P("wide", "narrow", None), P(), P(), P(), P()),
        check_vma=False,
    )
```

time: 67.8 us -> 60.7 us (0.90)
  Pallas kernels: 67 us -> 59.9 us
    pallas_call x1, Pallas kernels: 66.1 us -> 59 us  [everything(): pl.pallas_call(kernel, out_shape=(pltpu.VMEM((128, 256), B16), pltpu.VMEM...]
where the time goes in v4:
time: 60.7 us; the launch traced here: 60.5 us
  Pallas kernels  59.9 us (99%)
  between operations  0.64 us (1%)
    pallas_call x1, Pallas kernels, everything(): pl.pallas_call(kernel, out_shape=(pltpu.VMEM((128, 256), B16), pltpu.VMEM...  59 us

profile of v4, /device:TPU:1, one launch (start us, length us, event | category | flops | bytes accessed | tf_op | source)
XLA Modules:
  0.0 60.5 jit_solution(221480684376624962)
XLA Ops:
  0.6 59.0 %shard_map.110 = (bf16[128,256]{1,0:T(8,128)(2,1)S(1)}, f32[64,256]{1,0:T(8,128)S(1)}, f32[2,32]{1,0:T(2,128)S(1)}, f32[2,256]{1,0:T(2,128)S(1)}, f32[1024,128]{1,0:T(8,128)S(1)}) custom-call(bf16[128,256]{1,0:T(8,128)(2,1)} %bitcast.10, bf16[8,64,128]{2,1,0:T(8,128)(2,1)} %pair_hbm.1, f32[1,256]{1,0:T(1,128)} %bitcast.12, f32[1,256]{1,0:T(1,128)} %bitcast.13, ...), custom_call_target="tpu_custom_call" | custom-call | tf_op jit(solution)/shard_map/pallas_call | solution.py:547
  59.6 0.9 %shard_map.111 = (bf16[128,256]{1,0:T(8,128)(2,1)}, f32[64,256]{1,0:T(8,128)}, f32[2,32]{1,0:T(2,128)}, f32[2,256]{1,0:T(2,128)}, f32[1024,128]{1,0:T(8,128)}) custom-call(bf16[128,256]{1,0:T(8,128)(2,1)S(1)} %get-tuple-element.15.refs_0_, f32[64,256]{1,0:T(8,128)S(1)} %get-tuple-element.16.refs_1_, f32[2,32]{1,0:T(2,128)S(1)} %get-tuple-element.17.refs_2_, ...), custom_call_target="tpu_custom_call" | custom-call | tf_op jit(solution)/shard_map/pallas_call | solution.py:518

commit v5 on v4

--- a/solution.py
+++ b/solution.py
@@ -7,13 +7,13 @@
 
 F32, B16 = jnp.float32, jnp.bfloat16
 MESH_ID = pl.DeviceIdType.MESH
-OFFSETS = (4, 3, 5, 2, 6, 1, 7)
-STAGES = 20
+OFFSETS = {"depth": (4, 3, 5, 2, 6, 1, 7), "narrow": (4, 3, 5, 2, 6, 1, 7), "plane": (6, 5, 7, 4, 2, 1, 3)}
+STAGES = 22
 SEQUENCES = 128
 (
     ROW_DEPTH, COL_DEPTH, ROW_PAIR, COL_PLANE, COLG_PLANE, ROWG_PAIR, BIG_PLANE, ROWG_DEPTH, COLG_DEPTH,
     BIG_DEPTH, SMALL_PLANE, BIG_NARROW, SMALL_DEPTH, BIG_BACK, SMALL_NARROW, BIG_OUT, SMALL_OUT,
-    PAIR_HALF, ROW_CORE, ROWG_CORE,
+    PAIR_HALF, ROW_CORE, ROWG_CORE, BIG_CORE, BIG_JOIN,
 ) = range(STAGES)
 
 
@@ -37,16 +37,18 @@
 
 
 def kernel(
-    x_ref, pair_hbm, gain_ref, shift_ref, weight_ref, bias_ref, out_weight_hbm,
+    x_hbm, pair_hbm, gain_hbm, shift_hbm, weight_hbm, bias_hbm, out_weight_hbm,
     align_out, proj_out, bias_out, norm_out, weight_out,
+    x_ref, gain_ref, shift_ref, weight_ref, bias_ref,
     normed, scaled, scaled32, inverse, row_tmp,
     row_send, col_send, row_got, col_got, col_wide, row_next, col_next,
     row_pair, col_plane, pair_ref, pair_tile, out_weight_ref, pair_two, weight32, weight_order, upstream, rows, rows_t, outer,
     colg_send, colg_got, rowg_acc, rowg_core, rowg_sum, rowg_send, rowg_got, rowg_next, rowg_depth, rowg,
     colg_wide, colg_next, colg_depth, scaled_grad,
-    big_send, big_plane, big_part, big_depth, big_two, big_narrow, big_three, big_back, big_half, big_all,
+    big_send, big_core, big_one, big_depth, big_part, big_plane, big_two, big_narrow, big_three, big_back, big_half,
+    big_most, big_rest,
     small_in, small_plane, small_part, small_depth, small_two, small_narrow, small_three, small_all,
-    send_sem, recv_sem, local_sem,
+    send_sem, recv_sem, local_sem, ready,
 ):
     wide = lax.axis_index("wide")
     narrow = lax.axis_index("narrow")
@@ -57,10 +59,14 @@
     lead = plane % 2 == narrow % 2
     follow = plane % 2 != narrow % 2
     barrier = pltpu.get_barrier_semaphore()
-    fetch_pair = pltpu.make_async_copy(pair_hbm, pair_ref, local_sem.at[0])
-    fetch_weight = pltpu.make_async_copy(out_weight_hbm, out_weight_ref, local_sem.at[1])
-    fetch_pair.start()
-    fetch_weight.start()
+    inputs = (
+        (x_hbm, x_ref), (gain_hbm, gain_ref), (shift_hbm, shift_ref), (weight_hbm, weight_ref), (bias_hbm, bias_ref),
+        (pair_hbm, pair_ref), (out_weight_hbm, out_weight_ref),
+    )
+    fetches = [pltpu.make_async_copy(a, b, local_sem.at[k]) for k, (a, b) in enumerate(inputs)]
+    for c in fetches:
+        c.start()
+    fetch_pair, fetch_weight = fetches[5:]
     place = {"plane": plane, "depth": depth, "narrow": narrow}
 
     def peer(kind, k):
@@ -80,28 +86,12 @@
         pl.semaphore_signal(barrier, 1, device_id=device, device_id_type=MESH_ID)
 
     for kind in ("plane", "depth", "narrow"):
-        for d in OFFSETS:
+        for d in OFFSETS[kind]:
             greet(peer(kind, (place[kind] + d) % 8))
-    for d in range(1, 4):
-        greet(holder(d))
-
-    @pl.when(lead)
-    def _():
-        for d in range(1, 8):
-            greet(source(d))
-
-    @pl.when(lead & other_pair)
-    def _():
-        greet(source(0))
-
-    @pl.when(other_pair)
-    def _():
-        greet(holder(0))
-
     def copies(stage, kind, give, target, size=1):
         me = place[kind]
         lead = pl.ds(pl.multiple_of(me * size, size), size) if size > 1 else me
-        for d in OFFSETS:
+        for d in OFFSETS[kind]:
             k = (me + d) % 8
             pltpu.make_async_remote_copy(
                 src_ref=give(k),
@@ -140,6 +130,8 @@
         pl.when(own_pair)(lambda: what(True))
         pl.when(other_pair)(lambda: what(False))
 
+    for c in fetches[:5]:
+        c.wait()
     value = x_ref[...].astype(F32)
     centre = value - jnp.mean(value, axis=-1, keepdims=True)
     inv = lax.rsqrt(jnp.mean(centre * centre, axis=-1, keepdims=True) + 1e-05)
@@ -178,7 +170,10 @@
     fac_a, fac_b = col_fac[:16], col_fac[16:]
     col_send[0] = jnp.where(even_lane, fac_a, pltpu.roll(fac_b, 32, 1)).astype(B16)
     col_send[1] = jnp.where(even_lane, pltpu.roll(fac_a, 96, 1), fac_b).astype(B16)
-    pl.semaphore_wait(barrier, 25 + jnp.where(lead, 8, 0) - jnp.where(own_pair, 2, 0))
+    pl.semaphore_wait(barrier, 21)
+    for d in (2, 4, 6):
+        pl.semaphore_signal(ready, 1, device_id=(wide, (narrow + d) % 8), device_id_type=MESH_ID)
+
 
     def eight(ref, k):
         return ref.at[pl.ds(pl.multiple_of(k * 8, 8), 8)]
@@ -189,6 +184,30 @@
     mine = pl.ds(pl.multiple_of(depth * 8, 8), 8)
     row_got[mine, :] = row_send[pl.ds(pl.multiple_of(depth // 2 * 8, 8), 8), :]
     col_got[depth] = col_send[parity]
+    fetch_weight.wait()
+    weight32[...] = out_weight_ref[...].astype(F32)
+    for b in range(8):
+        for c in range(4):
+            q = c % 2 * 16 + b * 2 + c // 2
+            weight_order[pl.ds((b * 4 + c) * 32, 32), :] = weight32[pl.ds(q, 32, stride=32), :].astype(B16)
+
+    finish(row_depth_c)
+    for g in range(4):
+        both = [row_got[pl.ds(r * 4 + g, 8, stride=8), :] for r in range(2)]
+        row_next[g] = jnp.concatenate(both, axis=0).astype(B16)
+
+    pl.semaphore_wait(ready, 3)
+    for d in (2, 1, 3):
+        sent(ROW_PAIR, holder(d), row_next, row_pair.at[plane]).start()
+
+    @pl.when(other_pair)
+    def _():
+        sent(ROW_PAIR, holder(0), row_next, row_pair.at[plane]).start()
+
+    @pl.when(own_pair)
+    def _():
+        row_pair[plane] = row_next[...]
+
     fetch_pair.wait()
     own_rows = pl.ds(pl.multiple_of(parity * 8, 8), 8)
     pair_half_c = pltpu.make_async_remote_copy(
@@ -201,29 +220,6 @@
     )
     pair_half_c.start()
     pair_tile[own_rows] = pair_ref[:, pl.ds(pl.multiple_of(parity * 32, 32), 32), :]
-
-    fetch_weight.wait()
-    weight32[...] = out_weight_ref[...].astype(F32)
-    for b in range(8):
-        for c in range(4):
-            q = c % 2 * 16 + b * 2 + c // 2
-            weight_order[pl.ds((b * 4 + c) * 32, 32), :] = weight32[pl.ds(q, 32, stride=32), :].astype(B16)
-
-    finish(row_depth_c)
-    for g in range(4):
-        both = [row_got[pl.ds(r * 4 + g, 8, stride=8), :] for r in range(2)]
-        row_next[g] = jnp.concatenate(both, axis=0).astype(B16)
-
-    for d in range(1, 4):
-        sent(ROW_PAIR, holder(d), row_next, row_pair.at[plane]).start()
-
-    @pl.when(other_pair)
-    def _():
-        sent(ROW_PAIR, holder(0), row_next, row_pair.at[plane]).start()
-
-    @pl.when(own_pair)
-    def _():
-        row_pair[plane] = row_next[...]
 
     finish(col_depth_c)
     col_wide[...] = col_got[...].astype(F32).reshape(128, 128)
@@ -340,8 +336,15 @@
         for k in range(4):
             for c in range(4):
                 big_send[g * 4 + k, pl.ds(c * 32, 32), :] = res[k * 32 : k * 32 + 32, c * 128 : c * 128 + 128]
-    big_plane_c = copies(BIG_PLANE, "plane", lambda k: big_send.at[k], big_plane)
-    big_plane[plane] = big_send[plane]
+    core = narrow % 2
+    own_half = pl.ds(pl.multiple_of(core * 64, 64), 64)
+    other_half = pl.ds(pl.multiple_of(64 - core * 64, 64), 64)
+    big_core_c = sent(BIG_CORE, partner, big_send.at[:, other_half], big_core)
+    big_core_c.start()
+    big_core_c.wait()
+    big_one[...] = (big_send[:, own_half, :].astype(F32) + big_core[...].astype(F32)).astype(B16)
+    big_depth_c = copies(BIG_DEPTH, "depth", lambda k: big_one.at[k], big_depth)
+    big_depth[depth] = big_one[depth]
 
     def came_rowg(own):
         part = rowg_got.at[pl.ds(0, 3 if own else 4)]
@@ -370,10 +373,10 @@
     colg_depth_c = copies(COLG_DEPTH, "depth", lambda k: colg_next.at[k], colg_depth)
     colg_depth[depth] = colg_next[depth]
 
-    finish(big_plane_c)
-    big_part[...] = total(big_plane).astype(B16).reshape(8, 16, 128)
-    big_depth_c = copies(BIG_DEPTH, "depth", lambda k: big_part.at[k], big_depth)
-    big_depth[depth] = big_part[depth]
+    finish(big_depth_c)
+    big_part[...] = total(big_depth).astype(B16).reshape(8, 8, 128)
+    big_plane_c = copies(BIG_PLANE, "plane", lambda k: big_part.at[k], big_plane)
+    big_plane[plane] = big_part[plane]
 
     finish(rowg_depth_c)
     for g in range(4):
@@ -445,10 +448,14 @@
     )
     align_out[...] = align.astype(B16)
 
-    finish(big_depth_c)
-    big_two[...] = total(big_depth).astype(B16)
-    big_narrow_c = copies(BIG_NARROW, "narrow", lambda k: big_two, big_narrow)
-    big_narrow[narrow] = big_two[...]
+    finish(big_plane_c)
+    big_two[...] = total(big_plane).astype(B16)
+    chip = narrow // 2
+    for d in (2, 1, 3):
+        sent(BIG_NARROW, (wide, (narrow + 2 * d) % 8), big_two, big_narrow.at[chip]).start()
+    big_narrow[chip] = big_two[...]
+    three = big_narrow.at[pl.ds(0, 3)]
+    big_narrow_c = sent(BIG_NARROW, partner, three, three)
 
     finish(small_plane_c)
     small_part[...] = total(small_plane).astype(B16)
@@ -456,9 +463,12 @@
     small_depth[depth] = small_part[...]
 
     finish(big_narrow_c)
-    big_three[...] = total(big_narrow).astype(B16)
-    big_back_c = copies(BIG_BACK, "depth", lambda k: big_three, big_back)
-    big_back[depth] = big_three[...]
+    big_sum = big_narrow[0].astype(F32)
+    for k in range(1, 4):
+        big_sum = big_sum + big_narrow[k].astype(F32)
+    big_three[...] = big_sum.astype(B16)
+    big_back_c = copies(BIG_BACK, "plane", lambda k: big_three, big_back)
+    big_back[plane] = big_three[...]
 
     finish(small_depth_c)
     small_two[...] = total(small_depth).astype(B16)
@@ -466,9 +476,9 @@
     small_narrow[narrow] = small_two[...]
 
     finish(big_back_c)
-    big_half[...] = big_back[...].reshape(128, 128)
-    big_out_c = copies(BIG_OUT, "plane", lambda k: big_half, big_all)
-    big_all[plane] = big_half[...]
+    big_half[...] = big_back[...].reshape(64, 128)
+    big_out_c = copies(BIG_OUT, "depth", lambda k: big_half, big_most)
+    big_most[depth] = big_half[...]
 
     finish(small_narrow_c)
     small_three[...] = total(small_narrow).astype(B16)
@@ -476,10 +486,18 @@
     small_all[plane] = small_three[...]
 
     finish(big_out_c)
-    for k in range(8):
-        for c in range(4):
-            piece = big_all[k, pl.ds(c * 32, 32), :].astype(F32)
-            weight_out[pl.ds(c % 2 * 16 + k * 2 + c // 2, 32, stride=32), :] = piece
+    big_join_c = sent(BIG_JOIN, partner, big_most, big_rest)
+    big_join_c.start()
+
+    def put_weight(ref, part):
+        for k in range(8):
+            for c in range(2):
+                piece = ref[k, pl.ds(c * 32, 32), :].astype(F32)
+                weight_out[pl.ds(c * 16 + k * 2 + part, 32, stride=32), :] = piece
+
+    put_weight(big_most, core)
+    big_join_c.wait()
+    put_weight(big_rest, 1 - core)
     @pl.when(lead)
     def _():
         sent(ROW_CORE, partner, row_pair, row_pair).wait_send()
@@ -528,6 +546,7 @@
     vmem = pl.BlockSpec(memory_space=pltpu.VMEM)
     hbm = pl.BlockSpec(memory_space=pl.ANY)
     scratch = [
+        ((128, 256), B16), ((1, 256), F32), ((1, 256), F32), ((64, 256), B16), ((2, 32), F32),
         ((128, 256), F32), ((128, 256), B16), ((2, 128, 128), F32), ((128, 128), F32), ((32, 128), F32),
         ((32, 128), F32), ((2, 16, 128), B16), ((64, 128), F32), ((8, 16, 128), B16), ((128, 128), F32),
         ((4, 16, 128), B16), ((8, 16, 128), B16),
@@ -538,9 +557,9 @@
         ((8, 4, 16, 128), B16),
         ((4, 4, 16, 128), B16), ((64, 128), F32), ((64, 128), F32), ((32, 128), F32),
         ((128, 128), F32), ((8, 16, 128), B16), ((8, 16, 128), B16), ((2, 128, 128), F32),
-        ((8, 128, 128), B16), ((8, 128, 128), B16), ((8, 16, 128), B16), ((8, 16, 128), B16), ((16, 128), B16),
-        ((8, 16, 128), B16), ((16, 128), B16), ((8, 16, 128), B16), ((128, 128), B16),
-        ((8, 128, 128), B16),
+        ((8, 128, 128), B16), ((8, 64, 128), B16), ((8, 64, 128), B16), ((8, 64, 128), B16), ((8, 8, 128), B16),
+        ((8, 8, 128), B16), ((8, 128), B16), ((4, 8, 128), B16), ((8, 128), B16), ((8, 8, 128), B16), ((64, 128), B16),
+        ((8, 64, 128), B16), ((8, 64, 128), B16),
         ((192, 128), F32), ((8, 24, 128), F32), ((24, 128), B16), ((8, 24, 128), B16), ((24, 128), B16),
         ((8, 24, 128), B16), ((24, 128), B16), ((8, 24, 128), B16),
     ]
@@ -553,10 +572,10 @@
             pltpu.VMEM((2, 256), F32),
             pltpu.VMEM((1024, 128), F32),
         ),
-        in_specs=[vmem, hbm, vmem, vmem, vmem, vmem, hbm],
+        in_specs=[hbm] * 7,
         out_specs=(vmem,) * 5,
         scratch_shapes=[pltpu.VMEM(shape, kind) for shape, kind in scratch]
-        + [pltpu.SemaphoreType.DMA((STAGES,)), pltpu.SemaphoreType.DMA((STAGES,)), pltpu.SemaphoreType.DMA((2,))],
+        + [pltpu.SemaphoreType.DMA((STAGES,)), pltpu.SemaphoreType.DMA((STAGES,)), pltpu.SemaphoreType.DMA((7,)), pltpu.SemaphoreType.REGULAR],
         compiler_params=pltpu.CompilerParams(
             collective_id=0, has_side_effects=True, vmem_limit_bytes=56 * 1024 * 1024
         ),

time: 60.7 us -> 59 us (0.972)
  Pallas kernels: 59.9 us -> 58.2 us
    pallas_call x1, Pallas kernels: 59 us -> 57.4 us  [everything(): pl.pallas_call(kernel, out_shape=(pltpu.VMEM((128, 256), B16), pltpu.VMEM...]
where the time goes in v5:
time: 59 us; the launch traced here: 58.9 us
  Pallas kernels  58.2 us (99%)
  between operations  0.64 us (1%)
    pallas_call x1, Pallas kernels, everything(): pl.pallas_call(kernel, out_shape=(pltpu.VMEM((128, 256), B16), pltpu.VMEM...  57.4 us

profile of v5, /device:TPU:1, one launch (start us, length us, event | category | flops | bytes accessed | tf_op | source)
XLA Modules:
  0.0 58.9 jit_solution(6755969849286169368)
XLA Ops:
  0.6 57.4 %shard_map.110 = (bf16[128,256]{1,0:T(8,128)(2,1)S(1)}, f32[64,256]{1,0:T(8,128)S(1)}, f32[2,32]{1,0:T(2,128)S(1)}, f32[2,256]{1,0:T(2,128)S(1)}, f32[1024,128]{1,0:T(8,128)S(1)}) custom-call(bf16[128,256]{1,0:T(8,128)(2,1)} %bitcast.10, bf16[8,64,128]{2,1,0:T(8,128)(2,1)} %pair_hbm.1, f32[1,256]{1,0:T(1,128)} %bitcast.12, f32[1,256]{1,0:T(1,128)} %bitcast.13, ...), custom_call_target="tpu_custom_call" | custom-call | tf_op jit(solution)/shard_map/pallas_call | solution.py:566
  58.0 0.9 %shard_map.111 = (bf16[128,256]{1,0:T(8,128)(2,1)}, f32[64,256]{1,0:T(8,128)}, f32[2,32]{1,0:T(2,128)}, f32[2,256]{1,0:T(2,128)}, f32[1024,128]{1,0:T(8,128)}) custom-call(bf16[128,256]{1,0:T(8,128)(2,1)S(1)} %get-tuple-element.15.refs_0_, f32[64,256]{1,0:T(8,128)S(1)} %get-tuple-element.16.refs_1_, f32[2,32]{1,0:T(2,128)S(1)} %get-tuple-element.17.refs_2_, ...), custom_call_target="tpu_custom_call" | custom-call | tf_op jit(solution)/shard_map/pallas_call | solution.py:536

commit v6 on v5

--- a/solution.py
+++ b/solution.py
@@ -8,12 +8,12 @@
 F32, B16 = jnp.float32, jnp.bfloat16
 MESH_ID = pl.DeviceIdType.MESH
 OFFSETS = {"depth": (4, 3, 5, 2, 6, 1, 7), "narrow": (4, 3, 5, 2, 6, 1, 7), "plane": (6, 5, 7, 4, 2, 1, 3)}
-STAGES = 22
+STAGES = 24
 SEQUENCES = 128
 (
     ROW_DEPTH, COL_DEPTH, ROW_PAIR, COL_PLANE, COLG_PLANE, ROWG_PAIR, BIG_PLANE, ROWG_DEPTH, COLG_DEPTH,
     BIG_DEPTH, SMALL_PLANE, BIG_NARROW, SMALL_DEPTH, BIG_BACK, SMALL_NARROW, BIG_OUT, SMALL_OUT,
-    PAIR_HALF, ROW_CORE, ROWG_CORE, BIG_CORE, BIG_JOIN,
+    PAIR_HALF, ROW_CORE, ROWG_CORE, BIG_CORE, BIG_JOIN, NORM_ROW, NORM_COL,
 ) = range(STAGES)
 
 
@@ -45,9 +45,10 @@
     row_pair, col_plane, pair_ref, pair_tile, out_weight_ref, pair_two, weight32, weight_order, upstream, rows, rows_t, outer,
     colg_send, colg_got, rowg_acc, rowg_core, rowg_sum, rowg_send, rowg_got, rowg_next, rowg_depth, rowg,
     colg_wide, colg_next, colg_depth, scaled_grad,
-    big_send, big_core, big_one, big_depth, big_part, big_plane, big_two, big_narrow, big_three, big_back, big_half,
-    big_most, big_rest,
+    big_send, big_core, big_one, big_depth, big_part, big_plane, big_two, big_narrow, big_three, big_back,
+    big_all,
     small_in, small_plane, small_part, small_depth, small_two, small_narrow, small_three, small_all,
+    norm_tmp, norm_row_send, norm_col_send, norm_row, norm_col, norm_two,
     send_sem, recv_sem, local_sem, ready,
 ):
     wide = lax.axis_index("wide")
@@ -64,9 +65,6 @@
         (pair_hbm, pair_ref), (out_weight_hbm, out_weight_ref),
     )
     fetches = [pltpu.make_async_copy(a, b, local_sem.at[k]) for k, (a, b) in enumerate(inputs)]
-    for c in fetches:
-        c.start()
-    fetch_pair, fetch_weight = fetches[5:]
     place = {"plane": plane, "depth": depth, "narrow": narrow}
 
     def peer(kind, k):
@@ -85,9 +83,17 @@
     def greet(device):
         pl.semaphore_signal(barrier, 1, device_id=device, device_id_type=MESH_ID)
 
-    for kind in ("plane", "depth", "narrow"):
+    def greet_all(kind):
         for d in OFFSETS[kind]:
             greet(peer(kind, (place[kind] + d) % 8))
+
+    greet_all("depth")
+    for c in fetches:
+        c.start()
+    fetch_pair, fetch_weight = fetches[5:]
+    greet_all("narrow")
+    greet_all("plane")
+
     def copies(stage, kind, give, target, size=1):
         me = place[kind]
         lead = pl.ds(pl.multiple_of(me * size, size), size) if size > 1 else me
@@ -236,7 +242,21 @@
 
     low32 = lane128 < 64
     even32 = group % 2 == 0
+    for c in range(2):
+        norm_tmp[c] = normed[:, pl.ds(c * 128, 128)]
+    for g in range(4):
+        one = jnp.concatenate([norm_tmp[c, pl.ds(g, 32, stride=4), :] for c in range(2)], axis=1)
+        for k in range(4):
+            rs = [one[r * 16 + k * 4 : r * 16 + k * 4 + 4] for r in range(2)]
+            norm_row_send[k, g] = jnp.concatenate(rs, axis=0).astype(B16)
+    for h in range(2):
+        for r in range(2):
+            norm_col_send[h, pl.ds(r * 32, 32), :] = normed[pl.ds(r * 64 + h * 32, 32), :].astype(B16)
     pair_half_c.wait()
+    norm_row_c = copies(NORM_ROW, "depth", lambda k: norm_row_send.at[k // 2], norm_row)
+    norm_col_c = copies(NORM_COL, "depth", lambda k: norm_col_send.at[k % 2], norm_col)
+    norm_row[depth] = norm_row_send[depth // 2]
+    norm_col[depth] = norm_col_send[parity]
 
     def up(t, _):
         tile = pair_tile[...].reshape(512, 128)
@@ -276,19 +296,6 @@
         for_own(came)
         sent(ROW_CORE, partner, row_pair, row_pair).start()
 
-    @pl.when(follow)
-    def _():
-        sent(ROW_CORE, partner, row_pair, row_pair).wait_recv()
-
-    for g in range(4):
-        rows[:, pl.ds(g * 128, 128)] = row_pair[:, g].reshape(128, 128)
-    for t in range(4):
-        r = (dot(rows[...], upstream[t], (1, 0)) * (1.0 / SEQUENCES)).astype(B16)
-        for h in range(2):
-            colg_send[:, t * 2 + h] = r[:, h * 128 : h * 128 + 128].reshape(8, 16, 128)
-    colg_plane_c = copies(COLG_PLANE, "plane", lambda k: colg_send.at[k], colg_got)
-    colg_got[plane] = colg_send[plane]
-    rows_t[...] = rows[...].astype(F32).T.astype(B16)
     finish(col_plane_c)
 
     def col_tile(t):
@@ -307,12 +314,14 @@
     @pl.when(follow)
     def _():
         sent(ROWG_CORE, partner, rowg_send, rowg_core).start()
-
+        sent(ROW_CORE, partner, row_pair, row_pair).wait_recv()
+
+    for g in range(4):
+        rows[:, pl.ds(g * 128, 128)] = row_pair[:, g].reshape(128, 128)
     for t in range(4):
-        o = (dot(rows_t[...], col_tile(t), (1, 0)) * (1.0 / SEQUENCES)).astype(B16)
+        r = (dot(rows[...], upstream[t], (1, 0)) * (1.0 / SEQUENCES)).astype(B16)
         for h in range(2):
-            for i in range(16):
-                outer[t * 2 + h, :, pl.ds(i * 128, 128)] = o[i * 32 : i * 32 + 32, h * 128 : h * 128 + 128]
+            colg_send[:, t * 2 + h] = r[:, h * 128 : h * 128 + 128].reshape(8, 16, 128)
 
     @pl.when(lead)
     def _():
@@ -331,6 +340,15 @@
     def _():
         rowg_got[narrow // 2] = rowg_sum[plane]
 
+    colg_plane_c = copies(COLG_PLANE, "plane", lambda k: colg_send.at[k], colg_got)
+    colg_got[plane] = colg_send[plane]
+    rows_t[...] = rows[...].astype(F32).T.astype(B16)
+
+    for t in range(4):
+        o = (dot(rows_t[...], col_tile(t), (1, 0)) * (1.0 / SEQUENCES)).astype(B16)
+        for h in range(2):
+            for i in range(16):
+                outer[t * 2 + h, :, pl.ds(i * 128, 128)] = o[i * 32 : i * 32 + 32, h * 128 : h * 128 + 128]
     for g in range(2):
         res = dot(outer[pl.ds(g * 4, 4)].reshape(128, 2048), pair_two[...], (1, 0)).astype(B16)
         for k in range(4):
@@ -373,20 +391,69 @@
     colg_depth_c = copies(COLG_DEPTH, "depth", lambda k: colg_next.at[k], colg_depth)
     colg_depth[depth] = colg_next[depth]
 
+    finish(norm_row_c)
+    part_row = rowg_next[...]
+    part_row_b = part_row.astype(B16)
+    from_row = jnp.zeros((32, 256), F32)
+    for g in range(4):
+        near = norm_row[:, g].astype(F32).reshape(64, 256).astype(B16)
+        from_row = from_row + dot(part_row_b, near, (0, 0))[g * 32 : g * 32 + 32]
+    row_fold = jnp.sum(part_row, axis=0, keepdims=True)
+    row_fold = row_fold + pltpu.roll(row_fold, 32, 1) + pltpu.roll(row_fold, 64, 1) + pltpu.roll(row_fold, 96, 1)
+    finish(norm_col_c)
+    for k in range(8):
+        for r in range(2):
+            for h in range(2):
+                norm_two[pl.ds(k * 128 + r * 64 + h * 32, 32), :] = norm_col[k, pl.ds(r * 32, 32), :]
+    long = jnp.concatenate([colg_wide[pl.ds(k * 16, 16), :] for k in range(8)], axis=1)
+    even_long = lanes((16, 1024)) // 32 % 2 == 0
+    long2 = jnp.concatenate([jnp.where(even_long, long, 0.0), jnp.where(even_long, 0.0, long)], axis=0)
+    from_col = dot(long2.astype(B16), norm_two[...], (1, 0))
+    col_sum = jnp.sum(long2, axis=1, keepdims=True)
+    col_fold = jnp.sum(jnp.where(sub128 == lane128, col_sum, 0.0), axis=0, keepdims=True)
+    small_in[pl.ds(0, 32), :] = from_row[:, :128]
+    small_in[pl.ds(32, 32), :] = from_col[:, :128]
+    small_in[pl.ds(64, 32), :] = from_row[:, 128:]
+    small_in[pl.ds(96, 32), :] = from_col[:, 128:]
+    small_in[pl.ds(128, 64), :] = jnp.zeros((64, 128), F32)
+    small_in[pl.ds(128, 1), :] = row_fold
+    small_in[pl.ds(129, 1), :] = col_fold
+
+    def strip(ref, k):
+        return ref.at[pl.ds(pl.multiple_of(k * 24, 8), 24)]
+
+    small_plane_c = copies(SMALL_PLANE, "plane", lambda k: strip(small_in, k), small_plane)
+    small_plane[plane] = small_in[pl.ds(pl.multiple_of(plane * 24, 8), 24), :]
+
     finish(big_depth_c)
     big_part[...] = total(big_depth).astype(B16).reshape(8, 8, 128)
     big_plane_c = copies(BIG_PLANE, "plane", lambda k: big_part.at[k], big_plane)
     big_plane[plane] = big_part[plane]
 
+    finish(big_plane_c)
+    big_two[...] = total(big_plane).astype(B16)
+    chip = narrow // 2
+    for d in (2, 1, 3):
+        sent(BIG_NARROW, (wide, (narrow + 2 * d) % 8), big_two, big_narrow.at[chip]).start()
+    big_narrow[chip] = big_two[...]
+    three = big_narrow.at[pl.ds(0, 3)]
+    big_narrow_c = sent(BIG_NARROW, partner, three, three)
+
+    finish(small_plane_c)
+    small_part[...] = total(small_plane).astype(B16)
+    small_depth_c = copies(SMALL_DEPTH, "depth", lambda k: small_part, small_depth)
+    small_depth[depth] = small_part[...]
+
     finish(rowg_depth_c)
     for g in range(4):
         for r in range(2):
             one = rowg_depth[pl.ds(g * 16 + r * 4, 4), :] + rowg_depth[pl.ds(g * 16 + 8 + r * 4, 4), :]
             rowg[pl.ds(r * 16 + g * 4, 4), :] = one
-    row_g = rowg[...]
-    row_gb = row_g.astype(B16)
-    row_fold = jnp.sum(row_g, axis=0, keepdims=True)
-    row_fold = row_fold + pltpu.roll(row_fold, 32, 1) + pltpu.roll(row_fold, 64, 1) + pltpu.roll(row_fold, 96, 1)
+    row_gb = rowg[...].astype(B16).astype(F32)
+    for g in range(4):
+        more = dot(jnp.where(group == g, row_gb, 0.0).astype(B16), w_row4, (1, 0))
+        for c in range(2):
+            scaled_grad[c, pl.ds(g, 32, stride=4), :] = more[:, c * 128 : c * 128 + 128]
     finish(colg_depth_c)
     half = []
     for h in range(2):
@@ -394,51 +461,15 @@
         for k in range(1, 4):
             one = one + colg_depth[k * 2 + h].astype(F32)
         half.append(one)
-    col_g = jnp.concatenate(
+    col_gb = jnp.concatenate(
         [
             jnp.where(even_lane, half[0], pltpu.roll(half[1], 32, 1)),
             jnp.where(even_lane, pltpu.roll(half[0], 96, 1), half[1]),
         ],
         axis=0,
-    )
-    col_gb = col_g.astype(B16)
-    col_sum = jnp.sum(col_g, axis=1, keepdims=True)
-    col_fold = jnp.sum(jnp.where(sub128 == lane128, col_sum, 0.0), axis=0, keepdims=True)
-    from_cols = dot(col_gb, w_col, (0, 0))
-    for c in range(2):
-        scaled_grad[c] = from_cols[:, c * 128 : c * 128 + 128]
-    proj_col = dot(col_gb, scaled[...], (1, 0))
-    proj_row4 = jnp.zeros((128, 256), F32)
-    for g in range(4):
-        masked = jnp.where(group == g, row_gb.astype(F32), 0.0).astype(B16)
-        more = dot(masked, w_row4, (1, 0))
-        for c in range(2):
-            spot = (c, pl.ds(g, 32, stride=4), slice(None))
-            scaled_grad[spot] = scaled_grad[spot] + more[:, c * 128 : c * 128 + 128]
-        proj_row4 = proj_row4 + dot(masked, every_fourth(g), (0, 0))
-    proj_row = proj_row4[0:32] + proj_row4[32:64] + proj_row4[64:96] + proj_row4[96:128]
-    grad = jnp.concatenate([scaled_grad[0], scaled_grad[1]], axis=1)
+    ).astype(B16)
+    grad = jnp.concatenate([scaled_grad[0], scaled_grad[1]], axis=1) + dot(col_gb, w_col, (0, 0))
     norm = normed[...]
-    gain_grad = jnp.sum(grad * norm, axis=0, keepdims=True)
-    shift_grad = jnp.sum(grad, axis=0, keepdims=True)
-    small_in[pl.ds(0, 32), :] = proj_row[:, :128]
-    small_in[pl.ds(32, 32), :] = proj_col[:, :128]
-    small_in[pl.ds(64, 32), :] = proj_row[:, 128:]
-    small_in[pl.ds(96, 32), :] = proj_col[:, 128:]
-    small_in[pl.ds(128, 64), :] = jnp.zeros((64, 128), F32)
-    small_in[pl.ds(128, 1), :] = gain_grad[:, :128]
-    small_in[pl.ds(129, 1), :] = gain_grad[:, 128:]
-    small_in[pl.ds(130, 1), :] = shift_grad[:, :128]
-    small_in[pl.ds(131, 1), :] = shift_grad[:, 128:]
-    small_in[pl.ds(132, 1), :] = row_fold
-    small_in[pl.ds(133, 1), :] = col_fold
-
-    def strip(ref, k):
-        return ref.at[pl.ds(pl.multiple_of(k * 24, 8), 24)]
-
-    small_plane_c = copies(SMALL_PLANE, "plane", lambda k: strip(small_in, k), small_plane)
-    small_plane[plane] = small_in[pl.ds(pl.multiple_of(plane * 24, 8), 24), :]
-
     inv = inverse[...][:, :1]
     gained = grad * gain_ref[...]
     align = inv * (
@@ -448,27 +479,14 @@
     )
     align_out[...] = align.astype(B16)
 
-    finish(big_plane_c)
-    big_two[...] = total(big_plane).astype(B16)
-    chip = narrow // 2
-    for d in (2, 1, 3):
-        sent(BIG_NARROW, (wide, (narrow + 2 * d) % 8), big_two, big_narrow.at[chip]).start()
-    big_narrow[chip] = big_two[...]
-    three = big_narrow.at[pl.ds(0, 3)]
-    big_narrow_c = sent(BIG_NARROW, partner, three, three)
-
-    finish(small_plane_c)
-    small_part[...] = total(small_plane).astype(B16)
-    small_depth_c = copies(SMALL_DEPTH, "depth", lambda k: small_part, small_depth)
-    small_depth[depth] = small_part[...]
 
     finish(big_narrow_c)
     big_sum = big_narrow[0].astype(F32)
     for k in range(1, 4):
         big_sum = big_sum + big_narrow[k].astype(F32)
     big_three[...] = big_sum.astype(B16)
-    big_back_c = copies(BIG_BACK, "plane", lambda k: big_three, big_back)
-    big_back[plane] = big_three[...]
+    big_back_c = copies(BIG_BACK, "depth", lambda k: big_three, big_back)
+    big_back[depth] = big_three[...]
 
     finish(small_depth_c)
     small_two[...] = total(small_depth).astype(B16)
@@ -476,28 +494,22 @@
     small_narrow[narrow] = small_two[...]
 
     finish(big_back_c)
-    big_half[...] = big_back[...].reshape(64, 128)
-    big_out_c = copies(BIG_OUT, "depth", lambda k: big_half, big_most)
-    big_most[depth] = big_half[...]
+    slot = core * 8 + plane
+    other = narrow + 1 - 2 * core
+    for d in OFFSETS["plane"]:
+        k = (plane + d) % 8
+        sent(BIG_OUT, (k * 8 + depth, other), big_back, big_all.at[slot]).start()
+        sent(BIG_OUT, (k * 8 + depth, narrow), big_back, big_all.at[slot]).start()
+    sent(BIG_OUT, partner, big_back, big_all.at[slot]).start()
+    big_all[slot] = big_back[...]
+    fifteen = big_all.at[pl.ds(0, 15)]
+    big_out_c = sent(BIG_OUT, partner, fifteen, fifteen)
 
     finish(small_narrow_c)
     small_three[...] = total(small_narrow).astype(B16)
     small_out_c = copies(SMALL_OUT, "plane", lambda k: small_three, small_all)
     small_all[plane] = small_three[...]
 
-    finish(big_out_c)
-    big_join_c = sent(BIG_JOIN, partner, big_most, big_rest)
-    big_join_c.start()
-
-    def put_weight(ref, part):
-        for k in range(8):
-            for c in range(2):
-                piece = ref[k, pl.ds(c * 32, 32), :].astype(F32)
-                weight_out[pl.ds(c * 16 + k * 2 + part, 32, stride=32), :] = piece
-
-    put_weight(big_most, core)
-    big_join_c.wait()
-    put_weight(big_rest, 1 - core)
     @pl.when(lead)
     def _():
         sent(ROW_CORE, partner, row_pair, row_pair).wait_send()
@@ -514,18 +526,30 @@
 
     finish(small_out_c)
     small = small_all[...].astype(F32).reshape(192, 128)
-    proj_out[:, pl.ds(0, 128)] = small[0:64]
-    proj_out[:, pl.ds(128, 128)] = small[64:128]
-    norm_out[0:1, pl.ds(0, 128)] = small[128:129]
-    norm_out[0:1, pl.ds(128, 128)] = small[129:130]
-    norm_out[1:2, pl.ds(0, 128)] = small[130:131]
-    norm_out[1:2, pl.ds(128, 128)] = small[131:132]
-    bias_out[...] = small[132:134, :32]
+    bias_out[...] = small[128:130, :32]
+    first = jnp.sum(jnp.where(sub128 == lane128, small[128:129], 0.0), axis=1, keepdims=True)
+    second = jnp.sum(jnp.where(sub128 == lane128, small[129:130], 0.0), axis=1, keepdims=True)
+    sums = jnp.concatenate([first, second], axis=0)
+    product = jnp.concatenate([small[0:64], small[64:128]], axis=1)
+    proj_out[...] = gain_ref[...] * product + shift_ref[...] * sums
+    both = weight_ref[...].astype(F32)
+    norm_out[0:1, :] = jnp.sum(both * product, axis=0, keepdims=True)
+    norm_out[1:2, :] = jnp.sum(both * sums, axis=0, keepdims=True)
+    finish(big_out_c)
+    for part in range(2):
+        for k in range(8):
+            slice_k = big_all[pl.ds(part * 8, 8), k].astype(F32).reshape(64, 128)
+            for c in range(2):
+                weight_out[pl.ds(c * 16 + k * 2 + part, 32, stride=32), :] = slice_k[c * 32 : c * 32 + 32]
 
 
 def put_kernel(*refs):
     sem = refs[10]
-    made = [pltpu.make_async_copy(refs[k], refs[5 + k], sem.at[k]) for k in range(5)]
+    made = []
+    for k in range(4):
+        part = pl.ds(k * 256, 256)
+        made.append(pltpu.make_async_copy(refs[4].at[part], refs[9].at[part], sem.at[4 + k]))
+    made += [pltpu.make_async_copy(refs[k], refs[5 + k], sem.at[k]) for k in range(4)]
     for c in made:
         c.start()
     for c in made:
@@ -538,7 +562,7 @@
         out_shape=tuple(jax.ShapeDtypeStruct(r.shape, r.dtype) for r in results),
         in_specs=[pl.BlockSpec(memory_space=pltpu.VMEM)] * 5,
         out_specs=(pl.BlockSpec(memory_space=pl.ANY),) * 5,
-        scratch_shapes=[pltpu.SemaphoreType.DMA((5,))],
+        scratch_shapes=[pltpu.SemaphoreType.DMA((8,))],
     )(*[pltpu.with_memory_space_constraint(r, pltpu.VMEM) for r in results])
 
 
@@ -558,10 +582,12 @@
         ((4, 4, 16, 128), B16), ((64, 128), F32), ((64, 128), F32), ((32, 128), F32),
         ((128, 128), F32), ((8, 16, 128), B16), ((8, 16, 128), B16), ((2, 128, 128), F32),
         ((8, 128, 128), B16), ((8, 64, 128), B16), ((8, 64, 128), B16), ((8, 64, 128), B16), ((8, 8, 128), B16),
-        ((8, 8, 128), B16), ((8, 128), B16), ((4, 8, 128), B16), ((8, 128), B16), ((8, 8, 128), B16), ((64, 128), B16),
-        ((8, 64, 128), B16), ((8, 64, 128), B16),
+        ((8, 8, 128), B16), ((8, 128), B16), ((4, 8, 128), B16), ((8, 128), B16), ((8, 8, 128), B16),
+        ((16, 8, 8, 128), B16),
         ((192, 128), F32), ((8, 24, 128), F32), ((24, 128), B16), ((8, 24, 128), B16), ((24, 128), B16),
         ((8, 24, 128), B16), ((24, 128), B16), ((8, 24, 128), B16),
+        ((2, 128, 128), F32), ((4, 4, 8, 256), B16), ((2, 64, 256), B16), ((8, 4, 8, 256), B16), ((8, 64, 256), B16),
+        ((1024, 256), B16),
     ]
     return pl.pallas_call(
         kernel,

time: 59 us -> 57.1 us (0.968)
  Pallas kernels: 58.2 us -> 56.3 us
    pallas_call x1, Pallas kernels: 57.4 us -> 55.4 us  [everything(): pl.pallas_call(kernel, out_shape=(pltpu.VMEM((128, 256), B16), pltpu.VMEM...]
where the time goes in v6:
time: 57.1 us; the launch traced here: 56.9 us
  Pallas kernels  56.3 us (99%)
  between operations  0.64 us (1%)
    pallas_call x1, Pallas kernels, everything(): pl.pallas_call(kernel, out_shape=(pltpu.VMEM((128, 256), B16), pltpu.VMEM...  55.4 us

profile of v6, /device:TPU:1, one launch (start us, length us, event | category | flops | bytes accessed | tf_op | source)
XLA Modules:
  0.0 56.9 jit_solution(6028629180091251509)
XLA Ops:
  0.6 55.4 %shard_map.110 = (bf16[128,256]{1,0:T(8,128)(2,1)S(1)}, f32[64,256]{1,0:T(8,128)S(1)}, f32[2,32]{1,0:T(2,128)S(1)}, f32[2,256]{1,0:T(2,128)S(1)}, f32[1024,128]{1,0:T(8,128)S(1)}) custom-call(bf16[128,256]{1,0:T(8,128)(2,1)} %bitcast.10, bf16[8,64,128]{2,1,0:T(8,128)(2,1)} %pair_hbm.1, f32[1,256]{1,0:T(1,128)} %bitcast.12, f32[1,256]{1,0:T(1,128)} %bitcast.13, ...), custom_call_target="tpu_custom_call" | custom-call | tf_op jit(solution)/shard_map/pallas_call | solution.py:592
  56.0 0.9 %shard_map.111 = (bf16[128,256]{1,0:T(8,128)(2,1)}, f32[64,256]{1,0:T(8,128)}, f32[2,32]{1,0:T(2,128)}, f32[2,256]{1,0:T(2,128)}, f32[1024,128]{1,0:T(8,128)}) custom-call(bf16[128,256]{1,0:T(8,128)(2,1)S(1)} %get-tuple-element.15.refs_0_, f32[64,256]{1,0:T(8,128)S(1)} %get-tuple-element.16.refs_1_, f32[2,32]{1,0:T(2,128)S(1)} %get-tuple-element.17.refs_2_, ...), custom_call_target="tpu_custom_call" | custom-call | tf_op jit(solution)/shard_map/pallas_call | solution.py:560

commit v7 on v6

--- a/solution.py
+++ b/solution.py
@@ -88,10 +88,10 @@
             greet(peer(kind, (place[kind] + d) % 8))
 
     greet_all("depth")
+    greet_all("narrow")
     for c in fetches:
         c.start()
     fetch_pair, fetch_weight = fetches[5:]
-    greet_all("narrow")
     greet_all("plane")
 
     def copies(stage, kind, give, target, size=1):
@@ -252,29 +252,35 @@
     for h in range(2):
         for r in range(2):
             norm_col_send[h, pl.ds(r * 32, 32), :] = normed[pl.ds(r * 64 + h * 32, 32), :].astype(B16)
+
+    def up_half(which):
+        tile = pair_tile[pl.ds(pl.multiple_of(which * 8, 8), 8)].reshape(256, 128)
+
+        def up(t, _):
+            for h in range(2):
+                w = weight_order[pl.ds(pl.multiple_of(t * 256 + h * 128, 128), 128), :]
+                res = dot(w, tile, (1, 1))
+                for i in range(2):
+                    a = [res[c * 32 : c * 32 + 32, i * 128 : i * 128 + 128] for c in range(4)]
+                    first = [jnp.where(low32, a[c], half_swap(a[c + 2])) for c in range(2)]
+                    second = [jnp.where(low32, half_swap(a[c]), a[c + 2]) for c in range(2)]
+                    out = []
+                    for f in (first, second):
+                        out.append(jnp.where(even32, f[0], pltpu.roll(f[1], 32, 1)))
+                        out.append(jnp.where(even32, pltpu.roll(f[0], 96, 1), f[1]))
+                    spot = pl.ds(pl.multiple_of(which * 256 + i * 128, 128), 128)
+                    upstream[t, spot, pl.ds(h * 128, 128)] = jnp.concatenate(out, axis=0).astype(B16)
+            return 0
+
+        lax.fori_loop(0, 4, up, 0)
+
+    up_half(parity)
     pair_half_c.wait()
     norm_row_c = copies(NORM_ROW, "depth", lambda k: norm_row_send.at[k // 2], norm_row)
+    norm_row[depth] = norm_row_send[depth // 2]
+    up_half(1 - parity)
     norm_col_c = copies(NORM_COL, "depth", lambda k: norm_col_send.at[k % 2], norm_col)
-    norm_row[depth] = norm_row_send[depth // 2]
     norm_col[depth] = norm_col_send[parity]
-
-    def up(t, _):
-        tile = pair_tile[...].reshape(512, 128)
-        for h in range(2):
-            w = weight_order[pl.ds(pl.multiple_of(t * 256 + h * 128, 128), 128), :]
-            res = dot(w, tile, (1, 1))
-            for i in range(4):
-                a = [res[c * 32 : c * 32 + 32, i * 128 : i * 128 + 128] for c in range(4)]
-                first = [jnp.where(low32, a[c], half_swap(a[c + 2])) for c in range(2)]
-                second = [jnp.where(low32, half_swap(a[c]), a[c + 2]) for c in range(2)]
-                out = []
-                for f in (first, second):
-                    out.append(jnp.where(even32, f[0], pltpu.roll(f[1], 32, 1)))
-                    out.append(jnp.where(even32, pltpu.roll(f[0], 96, 1), f[1]))
-                upstream[t, pl.ds(i * 128, 128), pl.ds(h * 128, 128)] = jnp.concatenate(out, axis=0).astype(B16)
-        return 0
-
-    lax.fori_loop(0, 4, up, 0)
 
     pair_two[...] = jnp.zeros((2048, 512), B16)
     for i in range(16):
@@ -498,17 +504,31 @@
     other = narrow + 1 - 2 * core
     for d in OFFSETS["plane"]:
         k = (plane + d) % 8
-        sent(BIG_OUT, (k * 8 + depth, other), big_back, big_all.at[slot]).start()
         sent(BIG_OUT, (k * 8 + depth, narrow), big_back, big_all.at[slot]).start()
-    sent(BIG_OUT, partner, big_back, big_all.at[slot]).start()
     big_all[slot] = big_back[...]
-    fifteen = big_all.at[pl.ds(0, 15)]
-    big_out_c = sent(BIG_OUT, partner, fifteen, fifteen)
+    seven = big_all.at[pl.ds(0, 7)]
+    big_out_c = sent(BIG_OUT, partner, seven, seven)
+
+    for d in OFFSETS["plane"]:
+        k = (plane + d) % 8
+        sent(BIG_JOIN, (k * 8 + depth, other), big_back, big_all.at[slot]).start()
+    sent(BIG_JOIN, partner, big_back, big_all.at[slot]).start()
+    eight_more = big_all.at[pl.ds(0, 8)]
+    big_join_c = sent(BIG_JOIN, partner, eight_more, eight_more)
 
     finish(small_narrow_c)
     small_three[...] = total(small_narrow).astype(B16)
     small_out_c = copies(SMALL_OUT, "plane", lambda k: small_three, small_all)
     small_all[plane] = small_three[...]
+
+    def put_weight(part):
+        for k in range(8):
+            slice_k = big_all[pl.ds(pl.multiple_of(part * 8, 8), 8), k].astype(F32).reshape(64, 128)
+            for c in range(2):
+                weight_out[pl.ds(c * 16 + k * 2 + part, 32, stride=32), :] = slice_k[c * 32 : c * 32 + 32]
+
+    finish(big_out_c)
+    put_weight(core)
 
     @pl.when(lead)
     def _():
@@ -535,12 +555,8 @@
     both = weight_ref[...].astype(F32)
     norm_out[0:1, :] = jnp.sum(both * product, axis=0, keepdims=True)
     norm_out[1:2, :] = jnp.sum(both * sums, axis=0, keepdims=True)
-    finish(big_out_c)
-    for part in range(2):
-        for k in range(8):
-            slice_k = big_all[pl.ds(part * 8, 8), k].astype(F32).reshape(64, 128)
-            for c in range(2):
-                weight_out[pl.ds(c * 16 + k * 2 + part, 32, stride=32), :] = slice_k[c * 32 : c * 32 + 32]
+    finish(big_join_c)
+    put_weight(1 - core)
 
 
 def put_kernel(*refs):

time: 57.1 us -> 56.9 us (level)
  no operation moved by 1% of the time
where the time goes in v7:
time: 56.9 us; the launch traced here: 56.8 us
  Pallas kernels  56.2 us (99%)
  between operations  0.64 us (1%)
    pallas_call x1, Pallas kernels, everything(): pl.pallas_call(kernel, out_shape=(pltpu.VMEM((128, 256), B16), pltpu.VMEM...  55.3 us

profile of v7, /device:TPU:1, one launch (start us, length us, event | category | flops | bytes accessed | tf_op | source)
XLA Modules:
  0.0 56.8 jit_solution(1686177210825433087)
XLA Ops:
  0.6 55.3 %shard_map.110 = (bf16[128,256]{1,0:T(8,128)(2,1)S(1)}, f32[64,256]{1,0:T(8,128)S(1)}, f32[2,32]{1,0:T(2,128)S(1)}, f32[2,256]{1,0:T(2,128)S(1)}, f32[1024,128]{1,0:T(8,128)S(1)}) custom-call(bf16[128,256]{1,0:T(8,128)(2,1)} %bitcast.10, bf16[8,64,128]{2,1,0:T(8,128)(2,1)} %pair_hbm.1, f32[1,256]{1,0:T(1,128)} %bitcast.12, f32[1,256]{1,0:T(1,128)} %bitcast.13, ...), custom_call_target="tpu_custom_call" | custom-call | tf_op jit(solution)/shard_map/pallas_call | solution.py:608
  55.9 0.9 %shard_map.111 = (bf16[128,256]{1,0:T(8,128)(2,1)}, f32[64,256]{1,0:T(8,128)}, f32[2,32]{1,0:T(2,128)}, f32[2,256]{1,0:T(2,128)}, f32[1024,128]{1,0:T(8,128)}) custom-call(bf16[128,256]{1,0:T(8,128)(2,1)S(1)} %get-tuple-element.15.refs_0_, f32[64,256]{1,0:T(8,128)S(1)} %get-tuple-element.16.refs_1_, f32[2,32]{1,0:T(2,128)S(1)} %get-tuple-element.17.refs_2_, ...), custom_call_target="tpu_custom_call" | custom-call | tf_op jit(solution)/shard_map/pallas_call | solution.py:576

commit v8 on v7

--- a/solution.py
+++ b/solution.py
@@ -47,7 +47,7 @@
     colg_wide, colg_next, colg_depth, scaled_grad,
     big_send, big_core, big_one, big_depth, big_part, big_plane, big_two, big_narrow, big_three, big_back,
     big_all,
-    small_in, small_plane, small_part, small_depth, small_two, small_narrow, small_three, small_all,
+    small_in, small_send, small_plane, small_part, small_depth, small_two, small_narrow, small_three, small_all,
     norm_tmp, norm_row_send, norm_col_send, norm_row, norm_col, norm_two,
     send_sem, recv_sem, local_sem, ready,
 ):
@@ -425,11 +425,9 @@
     small_in[pl.ds(128, 1), :] = row_fold
     small_in[pl.ds(129, 1), :] = col_fold
 
-    def strip(ref, k):
-        return ref.at[pl.ds(pl.multiple_of(k * 24, 8), 24)]
-
-    small_plane_c = copies(SMALL_PLANE, "plane", lambda k: strip(small_in, k), small_plane)
-    small_plane[plane] = small_in[pl.ds(pl.multiple_of(plane * 24, 8), 24), :]
+    small_send[...] = small_in[...].reshape(8, 24, 128).astype(B16)
+    small_plane_c = copies(SMALL_PLANE, "plane", lambda k: small_send.at[k], small_plane)
+    small_plane[plane] = small_send[plane]
 
     finish(big_depth_c)
     big_part[...] = total(big_depth).astype(B16).reshape(8, 8, 128)
@@ -600,7 +598,7 @@
         ((8, 128, 128), B16), ((8, 64, 128), B16), ((8, 64, 128), B16), ((8, 64, 128), B16), ((8, 8, 128), B16),
         ((8, 8, 128), B16), ((8, 128), B16), ((4, 8, 128), B16), ((8, 128), B16), ((8, 8, 128), B16),
         ((16, 8, 8, 128), B16),
-        ((192, 128), F32), ((8, 24, 128), F32), ((24, 128), B16), ((8, 24, 128), B16), ((24, 128), B16),
+        ((192, 128), F32), ((8, 24, 128), B16), ((8, 24, 128), B16), ((24, 128), B16), ((8, 24, 128), B16), ((24, 128), B16),
         ((8, 24, 128), B16), ((24, 128), B16), ((8, 24, 128), B16),
         ((2, 128, 128), F32), ((4, 4, 8, 256), B16), ((2, 64, 256), B16), ((8, 4, 8, 256), B16), ((8, 64, 256), B16),
         ((1024, 256), B16),

time: 56.9 us -> 56.9 us (level)
  no operation moved by 1% of the time
where the time goes in v8:
time: 56.9 us; the launch traced here: 56.8 us
  Pallas kernels  56.2 us (99%)
  between operations  0.64 us (1%)
    pallas_call x1, Pallas kernels, everything(): pl.pallas_call(kernel, out_shape=(pltpu.VMEM((128, 256), B16), pltpu.VMEM...  55.3 us

profile of v8, /device:TPU:1, one launch (start us, length us, event | category | flops | bytes accessed | tf_op | source)
XLA Modules:
  0.0 56.8 jit_solution(7198254678010927633)
XLA Ops:
  0.6 55.3 %shard_map.110 = (bf16[128,256]{1,0:T(8,128)(2,1)S(1)}, f32[64,256]{1,0:T(8,128)S(1)}, f32[2,32]{1,0:T(2,128)S(1)}, f32[2,256]{1,0:T(2,128)S(1)}, f32[1024,128]{1,0:T(8,128)S(1)}) custom-call(bf16[128,256]{1,0:T(8,128)(2,1)} %bitcast.10, bf16[8,64,128]{2,1,0:T(8,128)(2,1)} %pair_hbm.1, f32[1,256]{1,0:T(1,128)} %bitcast.12, f32[1,256]{1,0:T(1,128)} %bitcast.13, ...), custom_call_target="tpu_custom_call" | custom-call | tf_op jit(solution)/shard_map/pallas_call | solution.py:606
  55.9 0.9 %shard_map.111 = (bf16[128,256]{1,0:T(8,128)(2,1)}, f32[64,256]{1,0:T(8,128)}, f32[2,32]{1,0:T(2,128)}, f32[2,256]{1,0:T(2,128)}, f32[1024,128]{1,0:T(8,128)}) custom-call(bf16[128,256]{1,0:T(8,128)(2,1)S(1)} %get-tuple-element.15.refs_0_, f32[64,256]{1,0:T(8,128)S(1)} %get-tuple-element.16.refs_1_, f32[2,32]{1,0:T(2,128)S(1)} %get-tuple-element.17.refs_2_, ...), custom_call_target="tpu_custom_call" | custom-call | tf_op jit(solution)/shard_map/pallas_call | solution.py:574
